TPU v7x, 512 devices: a whole 4x4x16 slice. The times are simulated.
512 devices in a mesh: rows: 128 (over z, x, core), grp: 4 (over y).
Axes of the slice: x: 4, y: 4, z: 16, core: 2. Of those that a mesh axis runs over, the one named last changes fastest.
Arguments:
- features: bfloat16 [4, 196608, 128], P('grp', 'rows'), may hold values from -6 to 6
- length_scale: bfloat16 [4, 196608], P('grp', 'rows'), may hold values from 32 to 256
- prior: bfloat16 [4, 196608], P('grp', 'rows'), may hold values from 0.45 to 18
- partners: int32 [4, 1536, 16], P('grp', 'rows'), may hold values from 0 to 1535, as said below
- counts: int32 [4, 1536], P('grp', 'rows'), may hold values from 12 to 16
- projection: bfloat16 [128, 64], replicated, may hold values from -0.5 to 0.5
Outputs:
- first_basis: float32 [4, 64, 196608], P('grp', None, 'rows')
- embedding: float32 [4, 64, 196608], P('grp', None, 'rows')
Inputs may be any that keep to these rules, and one draw needn't show every extreme that they name: `partners`: slot 0 of each tile names the tile itself; slots 1 to 12 name tiles held by the same device; slots 13 onward name tiles held by other devices along rows in the same group. Tiles may repeat in a list. Over one device's tiles, slots 13 onward name tiles of any one other device at most 1 times, and exactly 1 times for some device.
All inputs are finite; a program needn't handle non-finite values.
Results may differ from a plain program's by a relative error of at most 0.0047.
Values may be sent and summed in bfloat16 or wider, within the bound.
A program may use at most 128 MiB of HBM per device.

v0:
```python
import jax
import jax.numpy as jnp
from jax import lax
from jax.sharding import PartitionSpec as P

NEAR = 13


def kernel_tiles(own_rows, own_norm, own_band, part_rows, part_norm, part_band, alive_mask):
    cross_products = jnp.einsum(
        "naf,nsbf->nsab", own_rows, part_rows, preferred_element_type=jnp.float32
    )
    distance = jnp.maximum(
        own_norm[:, None, :, None] + part_norm[:, :, None, :] - 2.0 * cross_products, 0.0
    )
    spread = (
        own_band.astype(jnp.float32)[:, None, :, None]
        + part_band.astype(jnp.float32)[:, :, None, :]
    )
    return jnp.where(alive_mask[:, :, None, None], jnp.exp(-distance / spread), 0.0)


def density_term(kernel, extras):
    return jnp.sum(kernel, axis=(1, 3))


def walk_term(kernel, extras):
    rounded = lax.optimization_barrier(kernel.astype(jnp.bfloat16))
    degree = jnp.sum(rounded.astype(jnp.float32) * extras[0][:, :, None, :], axis=(1, 3))
    product = jnp.einsum("nsab,nscb->nca", rounded, extras[1], preferred_element_type=jnp.float32)
    return (degree, product)


def apply_term(kernel, extras):
    rounded = kernel.astype(jnp.bfloat16)
    return jnp.einsum("nsab,nscb->nca", rounded, extras[0], preferred_element_type=jnp.float32)


def sweep_blocks(block_term, own_arrays, pool_arrays, slot_table, alive_table, block_size):
    tiles_dev = own_arrays[0].shape[0]

    def one_block(block_step):
        first_tile = block_step * block_size
        own_block = [
            lax.dynamic_slice_in_dim(member, first_tile, block_size, 0) for member in own_arrays
        ]
        slot_block = lax.dynamic_slice_in_dim(slot_table, first_tile, block_size, 0)
        alive_block = lax.dynamic_slice_in_dim(alive_table, first_tile, block_size, 0)
        gathered = [jnp.take(member, slot_block, axis=0) for member in pool_arrays]
        kernel = kernel_tiles(
            own_block[0],
            own_block[1],
            own_block[2],
            gathered[0],
            gathered[1],
            gathered[2],
            alive_block,
        )
        return block_term(kernel, gathered[3:])

    stacked = lax.map(one_block, jnp.arange(tiles_dev // block_size, dtype=jnp.int32))
    return jax.tree.map(
        lambda stacked_part: stacked_part.reshape((tiles_dev,) + stacked_part.shape[2:]), stacked
    )


def combined(
    block_term,
    own_arrays,
    near_extras,
    far_arrays,
    far_extras,
    near_table,
    far_table,
    alive_table,
    block_size,
):
    pool_arrays = tuple(
        (
            jnp.concatenate([near_member, far_member], axis=0)
            for near_member, far_member in zip(own_arrays + near_extras, far_arrays + far_extras)
        )
    )
    slot_table = jnp.concatenate([near_table, far_table + own_arrays[0].shape[0]], axis=1)
    return sweep_blocks(block_term, own_arrays, pool_arrays, slot_table, alive_table, block_size)


def orthonormal(raw_basis, total_rows):
    local_gram = jnp.einsum("nca,nda->cd", raw_basis, raw_basis, precision=lax.Precision.HIGHEST)
    gram_matrix = lax.psum(local_gram, ("rows", "grp")) / total_rows
    lower = jnp.linalg.cholesky(gram_matrix)
    identity = jnp.eye(gram_matrix.shape[0], dtype=jnp.float32)
    lower_inverse = lax.linalg.triangular_solve(lower, identity, left_side=True, lower=True)
    return jnp.einsum("dc,nca->nda", lower_inverse, raw_basis, precision=lax.Precision.HIGHEST)


def columns_first(tile_basis):
    return jnp.transpose(tile_basis, (1, 0, 2)).reshape(
        1, tile_basis.shape[1], tile_basis.shape[0] * tile_basis.shape[2]
    )


def shards(features, length_scale, prior, partners, counts, projection):
    tiles_dev = partners.shape[1]
    part_slots = partners.shape[2]
    tile_rows = features.shape[1] // tiles_dev
    feature_width = features.shape[2]
    column_count = projection.shape[1]
    nrows = lax.axis_size("rows")
    device_index = lax.axis_index("rows")
    own_rows = features[0].reshape(tiles_dev, tile_rows, feature_width)
    own_band = length_scale[0].reshape(tiles_dev, tile_rows)
    own_prior = prior[0].reshape(tiles_dev, tile_rows)
    own_norm = jnp.einsum("naf,naf->na", own_rows, own_rows, preferred_element_type=jnp.float32)
    partner_lists = partners[0]
    far_tiles = partner_lists[:, NEAR:].reshape(-1)
    far_count = far_tiles.shape[0]
    capacity = max(1, (3 * far_count + 2 * nrows - 3) // (2 * (nrows - 1)))
    near_table = partner_lists[:, :NEAR] - device_index * tiles_dev
    alive_table = jnp.arange(part_slots, dtype=jnp.int32)[None, :] < counts[0][:, None]
    block_size = 2
    owner_index = far_tiles // tiles_dev
    local_index = far_tiles % tiles_dev
    owner_hits = (owner_index[:, None] == jnp.arange(nrows, dtype=jnp.int32)[None, :]).astype(
        jnp.int32
    )
    slot_rank = jnp.sum((jnp.cumsum(owner_hits, axis=0) - owner_hits) * owner_hits, axis=1)
    wanted = jnp.zeros((nrows, capacity), jnp.int32).at[owner_index, slot_rank].set(local_index)
    requested = lax.all_to_all(wanted, "rows", split_axis=0, concat_axis=0, tiled=True)
    got_rows, got_band, got_prior = (
        lax.all_to_all(
            jnp.take(own_rows, requested, axis=0), "rows", split_axis=0, concat_axis=0, tiled=True
        ),
        lax.all_to_all(
            jnp.take(own_band, requested, axis=0), "rows", split_axis=0, concat_axis=0, tiled=True
        ),
        lax.all_to_all(
            jnp.take(own_prior, requested, axis=0), "rows", split_axis=0, concat_axis=0, tiled=True
        ),
    )
    far_rows = got_rows.reshape(nrows * capacity, tile_rows, feature_width)
    far_band = got_band.reshape(nrows * capacity, tile_rows)
    far_prior = got_prior.reshape(nrows * capacity, tile_rows)
    far_table = (owner_index * capacity + slot_rank).reshape(tiles_dev, part_slots - NEAR)
    far_norm = jnp.einsum("naf,naf->na", far_rows, far_rows, preferred_element_type=jnp.float32)
    own_arrays = (own_rows, own_norm, own_band)
    far_arrays = (far_rows, far_norm, far_band)
    density = combined(
        density_term, own_arrays, (), far_arrays, (), near_table, far_table, alive_table, block_size
    )
    own_inverse = 1.0 / density
    far_inverse = (
        lax.all_to_all(
            jnp.take(own_inverse, requested, axis=0).astype(jnp.bfloat16),
            "rows",
            split_axis=0,
            concat_axis=0,
            tiled=True,
        )
        .astype(jnp.float32)
        .reshape(nrows * capacity, tile_rows)
    )
    own_start = jnp.einsum("naf,fc->nca", own_rows, projection, preferred_element_type=jnp.float32)
    own_scaled = (own_start * (own_prior.astype(jnp.float32) * own_inverse)[:, None, :]).astype(
        jnp.bfloat16
    )
    far_start = jnp.einsum("naf,fc->nca", far_rows, projection, preferred_element_type=jnp.float32)
    far_scaled = (far_start * (far_prior.astype(jnp.float32) * far_inverse)[:, None, :]).astype(
        jnp.bfloat16
    )
    degree, product = combined(
        walk_term,
        own_arrays,
        (own_inverse, own_scaled),
        far_arrays,
        (far_inverse, far_scaled),
        near_table,
        far_table,
        alive_table,
        block_size,
    )
    total_rows = nrows * lax.axis_size("grp") * tiles_dev * tile_rows
    first_basis = orthonormal(product / degree[:, None, :], total_rows)
    own_next = (first_basis * own_inverse[:, None, :]).astype(jnp.bfloat16)
    far_next = lax.all_to_all(
        jnp.take(own_next, requested, axis=0), "rows", split_axis=0, concat_axis=0, tiled=True
    ).reshape(nrows * capacity, column_count, tile_rows)
    second = combined(
        apply_term,
        own_arrays,
        (own_next,),
        far_arrays,
        (far_next,),
        near_table,
        far_table,
        alive_table,
        block_size,
    )
    final_basis = orthonormal(second / degree[:, None, :], total_rows)
    return (columns_first(first_basis), columns_first(final_basis))


def solution(mesh):
    in_specs = (
        P("grp", "rows", None),
        P("grp", "rows"),
        P("grp", "rows"),
        P("grp", "rows", None),
        P("grp", "rows"),
        P(),
    )
    out_specs = (P("grp", None, "rows"), P("grp", None, "rows"))
    return jax.shard_map(shards, mesh=mesh, in_specs=in_specs, out_specs=out_specs, check_vma=False)
```

profile of v0, /device:TPU:1, one launch (start us, length us, event | category | flops | bytes accessed | tf_op | source)
XLA Modules:
  0.0 839.4 jit_solution(2037871099502354747)
XLA Ops:
  4.0 20.4 %all-to-all-start = ((s32[128,1,1]{2,1,0:T(1,128)}), s32[128,1,1]{2,1,0:T(1,128)S(1)}, u32[]{:S(2)}, u32[]{:S(2)}) async-start(s32[128,1,1]{2,1,0:T(1,128)} %copy.68), calls=%async_computation | async-start | bytes 131072 | tf_op jit(solution)/shard_map/all_to_all | solution.py:129
  25.8 13.4 %all-to-all-done = s32[128,1,1]{2,1,0:T(1,128)S(1)} async-done(((s32[128,1,1]{2,1,0:T(1,128)}), s32[128,1,1]{2,1,0:T(1,128)S(1)}, u32[]{:S(2)}, u32[]{:S(2)}) %all-to-all-start) | async-done | bytes 544 | tf_op jit(solution)/shard_map/all_to_all | solution.py:129
  39.2 2.3 reduce.9
  41.6 2.4 and_reduce_fusion
  43.9 2.4 reduce.7
  48.5 5.6 all-to-all-start.2
  54.2 3.0 gather_fusion.12
  57.2 4.6 fusion.70
  61.7 7.5 all-to-all-done.2
  69.2 9.3 %all-to-all-start.1 = ((bf16[128,1,128,128]{3,2,1,0:T(8,128)(2,1)}), bf16[128,1,128,128]{3,2,1,0:T(8,128)(2,1)}, u32[]{:S(2)}, u32[]{:S(2)}) async-start(bf16[128,1,128,128]{3,2,1,0:T(8,128)(2,1)} %fusion.70), calls=%async_computation.1 | async-start | bytes 8388608 | tf_op jit(solution)/shard_map/all_to_all | solution.py:131
  79.7 182.3 %all-to-all-done.1 = bf16[128,1,128,128]{3,2,1,0:T(8,128)(2,1)} async-done(((bf16[128,1,128,128]{3,2,1,0:T(8,128)(2,1)}), bf16[128,1,128,128]{3,2,1,0:T(8,128)(2,1)}, u32[]{:S(2)}, u32[]{:S(2)}) %all-to-all-start.1) | async-done | bytes 4194336 | tf_op jit(solution)/shard_map/all_to_all | solution.py:131
  262.1 4.6 pad_maximum_fusion
  266.7 4.4 fusion.69
  271.2 45.2 %while.32 = (s32[]{:T(128)}, f32[6,2,128]{2,1,0:T(2,128)S(1)}, s32[6]{0:T(128)S(1)}, pred[12,16]{1,0:T(8,128)(4,1)S(1)}, f32[12,128]{1,0:T(8,128)S(1)}, /*index=...) while((s32[]{:T(128)}, f32[6,2,128]{2,1,0:T(2,128)S(1)}, ...), condition=%wide.region_5.10_spmd, body=%wide.region_3.9_spmd.sunk | while | flops 139474112 | bytes 3365755 | solution.py:61
  273.8 3.0 gather_fusion
  281.3 3.0 gather_fusion
  288.8 3.0 gather_fusion
  296.4 3.0 gather_fusion
  303.9 3.0 gather_fusion
  311.4 3.0 gather_fusion
  317.8 13.1 %all-to-all-start.3 = ((bf16[128,1,128]{2,1,0:T(2,128)(2,1)}), bf16[128,1,128]{2,1,0:T(2,128)(2,1)S(1)}, u32[]{:S(2)}, u32[]{:S(2)}) async-start(bf16[128,1,128]{2,1,0:T(2,128)(2,1)} %copy.71), calls=%async_computation.3 | async-start | bytes 131072 | tf_op jit(solution)/shard_map/all_to_all | solution.py:153
  330.9 14.8 %all-to-all-done.3 = bf16[128,1,128]{2,1,0:T(2,128)(2,1)S(1)} async-done(((bf16[128,1,128]{2,1,0:T(2,128)(2,1)}), bf16[128,1,128]{2,1,0:T(2,128)(2,1)S(1)}, u32[]{:S(2)}, u32[]{:S(2)}) %all-to-all-start.3) | async-done | bytes 32800 | tf_op jit(solution)/shard_map/all_to_all | solution.py:153
  345.7 5.9 all-to-all-start.4
  352.0 14.5 %all-to-all-done.4 = bf16[128,1,128]{2,1,0:T(2,128)(2,1)S(1)} async-done(((bf16[128,1,128]{2,1,0:T(2,128)(2,1)}), bf16[128,1,128]{2,1,0:T(2,128)(2,1)S(1)}, u32[]{:S(2)}, u32[]{:S(2)}) %all-to-all-start.4) | async-done | bytes 32800 | tf_op jit(solution)/shard_map/all_to_all | solution.py:137
  366.6 3.8 fusion.72
  372.1 69.3 %while.33 = (s32[]{:T(128)}, f32[6,2,128]{2,1,0:T(2,128)S(1)}, f32[6,2,64,128]{3,2,1,0:T(8,128)S(1)}, s32[6]{0:T(128)S(1)}, pred[12,16]{1,0:T(8,128)(4,1)S(1)}, ...) while((s32[]{:T(128)}, f32[6,2,128]{2,1,0:T(2,128)S(1)}, ...), condition=%wide.region_8.14_spmd, body=%wide.region_6.13_spmd.sunk | while | flops 208422080 | bytes 8232599 | solution.py:61
  375.3 3.0 gather_fusion.3
  386.9 3.0 gather_fusion.3
  391.8 2.3 gather_fusion.7
  398.4 3.0 gather_fusion.3
  410.0 3.0 gather_fusion.3
  421.6 3.0 gather_fusion.3
  433.1 3.0 gather_fusion.3
  441.9 100.6 %psum.14 = f32[64,64]{0,1:T(8,128)S(1)} all-reduce(f32[64,64]{0,1:T(8,128)S(1)} %convolution_bitcast_fusion.4), channel_id=1, replica_groups=mesh['rows'=128,'grp'=4] {'rows','grp'}, use_global_device_ids=true, to_apply=%region_9.15 | all-reduce | flops 4096 | bytes 32768 | tf_op jit(solution)/shard_map/psum | solution.py:90
  542.7 5.8 cholesky.44
  549.8 4.9 custom-call.6
  558.1 9.4 %all-to-all-start.5 = ((bf16[128,1,64,128]{3,2,1,0:T(8,128)(2,1)}), bf16[128,1,64,128]{3,2,1,0:T(8,128)(2,1)S(1)}, u32[]{:S(2)}, u32[]{:S(2)}) async-start(bf16[128,1,64,128]{3,2,1,0:T(8,128)(2,1)} %fusion.71), calls=%async_computation.5 | async-start | bytes 4194304 | tf_op jit(solution)/shard_map/all_to_all | solution.py:185
  570.4 93.9 %all-to-all-done.5 = bf16[128,1,64,128]{3,2,1,0:T(8,128)(2,1)S(1)} async-done(((bf16[128,1,64,128]{3,2,1,0:T(8,128)(2,1)}), bf16[128,1,64,128]{3,2,1,0:T(8,128)(2,1)S(1)}, u32[]{:S(2)}, u32[]{:S(2)}) %all-to-all-start.5) | async-done | bytes 2097184 | tf_op jit(solution)/shard_map/all_to_all | solution.py:185
  666.0 57.1 %while.34 = (s32[]{:T(128)}, f32[6,2,64,128]{3,2,1,0:T(8,128)S(1)}, s32[6]{0:T(128)S(1)}, s32[12,16]{1,0:T(8,128)S(1)}, bf16[140,64,128]{2,1,0:T(8,128)(2,1)}, /...) while((s32[]{:T(128)}, f32[6,2,64,128]{3,2,1,0:T(8,128)S(1)}, ...), condition=%wide.region_13.21_spmd, body=%wide.region_12.20_spmd.sunk | while | flops 206845376 | bytes 5001731 | solution.py:61
  668.6 3.0 gather_fusion.8
  678.1 3.0 gather_fusion.8
  687.6 3.0 gather_fusion.8
  697.1 3.0 gather_fusion.8
  706.7 3.0 gather_fusion.8
  716.2 3.0 gather_fusion.8
  723.6 101.8 %psum.15 = f32[64,64]{0,1:T(8,128)S(1)} all-reduce(f32[64,64]{0,1:T(8,128)S(1)} %convolution_bitcast_fusion.2), channel_id=1, replica_groups=mesh['rows'=128,'grp'=4] {'rows','grp'}, use_global_device_ids=true, to_apply=%region_14.22 | all-reduce | flops 4096 | bytes 32768 | tf_op jit(solution)/shard_map/psum | solution.py:90
  825.6 5.8 cholesky.55
  832.8 4.9 custom-call.7
  (325 shorter events, 127.4 us)
Async XLA Ops:
  0.6 351.1 %copy-start = (bf16[128,64]{0,1:T(8,128)(2,1)S(1)}, bf16[128,64]{0,1:T(8,128)(2,1)}, u32[]{:S(2)}) copy-start(bf16[128,64]{0,1:T(8,128)(2,1)} %param.30) | copy-start | bytes 49156
  0.6 53.5 %copy-start.1 = (bf16[1,1536,128]{2,1,0:T(8,128)(2,1)S(1)}, bf16[1,1536,128]{2,1,0:T(8,128)(2,1)}, u32[]{:S(2)}) copy-start(bf16[1,1536,128]{2,1,0:T(8,128)(2,1)} %param.25) | copy-start | bytes 1179652
  4.0 35.2 %all-to-all-start = ((s32[128,1,1]{2,1,0:T(1,128)}), s32[128,1,1]{2,1,0:T(1,128)S(1)}, u32[]{:S(2)}, u32[]{:S(2)}) async-start(s32[128,1,1]{2,1,0:T(1,128)} %copy.68), calls=%async_computation | async-start | bytes 131072 | tf_op jit(solution)/shard_map/all_to_all | solution.py:129
  48.5 20.7 %all-to-all-start.2 = ((bf16[128,1,128]{2,1,0:T(2,128)(2,1)}), bf16[128,1,128]{2,1,0:T(2,128)(2,1)S(1)}, u32[]{:S(2)}, u32[]{:S(2)}) async-start(bf16[128,1,128]{2,1,0:T(2,128)(2,1)} %copy.70), calls=%async_computation.2 | async-start | bytes 131072 | tf_op jit(solution)/shard_map/all_to_all | solution.py:134
  61.7 17.2 %copy-start.2 = (s32[1,12]{1,0:T(1,128)S(1)}, s32[1,12]{1,0:T(1,128)}, u32[]{:S(2)}) copy-start(s32[1,12]{1,0:T(1,128)} %param.29) | copy-start | bytes 148
  69.2 192.9 %all-to-all-start.1 = ((bf16[128,1,128,128]{3,2,1,0:T(8,128)(2,1)}), bf16[128,1,128,128]{3,2,1,0:T(8,128)(2,1)}, u32[]{:S(2)}, u32[]{:S(2)}) async-start(bf16[128,1,128,128]{3,2,1,0:T(8,128)(2,1)} %fusion.70), calls=%async_computation.1 | async-start | bytes 8388608 | tf_op jit(solution)/shard_map/all_to_all | solution.py:131
  317.8 28.0 %all-to-all-start.3 = ((bf16[128,1,128]{2,1,0:T(2,128)(2,1)}), bf16[128,1,128]{2,1,0:T(2,128)(2,1)S(1)}, u32[]{:S(2)}, u32[]{:S(2)}) async-start(bf16[128,1,128]{2,1,0:T(2,128)(2,1)} %copy.71), calls=%async_computation.3 | async-start | bytes 131072 | tf_op jit(solution)/shard_map/all_to_all | solution.py:153
  345.7 20.8 %all-to-all-start.4 = ((bf16[128,1,128]{2,1,0:T(2,128)(2,1)}), bf16[128,1,128]{2,1,0:T(2,128)(2,1)S(1)}, u32[]{:S(2)}, u32[]{:S(2)}) async-start(bf16[128,1,128]{2,1,0:T(2,128)(2,1)} %copy.72), calls=%async_computation.4 | async-start | bytes 131072 | tf_op jit(solution)/shard_map/all_to_all | solution.py:137
  558.1 106.2 %all-to-all-start.5 = ((bf16[128,1,64,128]{3,2,1,0:T(8,128)(2,1)}), bf16[128,1,64,128]{3,2,1,0:T(8,128)(2,1)S(1)}, u32[]{:S(2)}, u32[]{:S(2)}) async-start(bf16[128,1,64,128]{3,2,1,0:T(8,128)(2,1)} %fusion.71), calls=%async_computation.5 | async-start | bytes 4194304 | tf_op jit(solution)/shard_map/all_to_all | solution.py:185
where the time goes:
time: 850 us; the launch traced here: 839 us
  waiting for transfers between devices  326 us (38%)
  blocking collectives  202 us (24%)
  local copies, waits for them, and re-layouts  133 us (16%)
  starting transfers between devices  63.9 us (8%)
  other arithmetic  60.4 us (7%)
  matrix products  40 us (5%)
  loops' own time  11.9 us (1%)
    psum x2, blocking collectives, orthonormal(): gram_matrix = lax.psum(local_gram, ('rows', 'grp')) / total_rows  202 us
    all_to_all x1, waiting for transfers between devices, shards(): lax.all_to_all(jnp.take(own_rows, requested, axis=0), 'rows', split_axis=...  182 us
    gather x72, local copies, waits for them, and re-layouts, one_block(): gathered = [jnp.take(member, slot_block, axis=0) for member in pool_arrays]  107 us
    all_to_all x1, waiting for transfers between devices, shards(): lax.all_to_all(jnp.take(own_next, requested, axis=0), 'rows', split_axis=...  93.9 us
    dot_general x12, matrix products, kernel_tiles(): jnp.einsum('naf,nsbf->nsab', own_rows, part_rows, preferred_element_type=...  21.5 us
    all_to_all x1, starting transfers between devices, shards(): lax.all_to_all(wanted, 'rows', split_axis=0, concat_axis=0, tiled=True)  20.4 us
  transfers between devices with their start and end apart: 6, of which 6 were waited for; matrix products, arithmetic and copies ran while one was open for 2% of the time, Pallas kernels for 0%

commit v1 on v0

v1 whole, which is shorter than its diff:
```python
import functools

import jax
import jax.numpy as jnp
from jax import lax
from jax.experimental import pallas as pl
from jax.experimental.pallas import tpu as pltpu
from jax.sharding import PartitionSpec as P

NEAR = 13
PLANE = 8
MESH = pl.DeviceIdType.MESH
VMEM = pl.BlockSpec(memory_space=pltpu.VMEM)
SMEM = pl.BlockSpec(memory_space=pltpu.SMEM)


def nt_dot(left, right, precision=None):
    return lax.dot_general(
        left,
        right,
        (((1,), (1,)), ((), ())),
        precision=precision,
        preferred_element_type=jnp.float32,
    )


def slot_tile(table, tile, slot, slots, tiles):
    if slot < NEAR:
        return table[tile * slots + slot]
    return tiles + tile * (slots - NEAR) + (slot - NEAR)


def kernel_body(tiles, slots, table, counts, pool, band, kernel_half, inverse, norm_b, band_b, norm_a):
    size = pool.shape[1]

    def prepare(index, carry):
        rows = pool[index].astype(jnp.float32)
        norm = jnp.sum(rows * rows, axis=1, keepdims=True)
        wide = jnp.broadcast_to(-norm, (size, size))
        norm_b[index] = wide
        band_b[index] = jnp.transpose(jnp.broadcast_to(band[index], (size, size)))

        @pl.when(index < tiles)
        def _():
            norm_a[index] = jnp.transpose(wide)[0:1, :]

        return carry

    lax.fori_loop(0, pool.shape[0], prepare, 0)

    def one_tile(tile, carry):
        doubled = pool[tile] * jnp.bfloat16(2)
        own_norm = norm_a[tile]
        own_band = band[tile]
        live = counts[tile]
        total = jnp.zeros((8, size), jnp.float32)
        for slot in range(slots):
            index = slot_tile(table, tile, slot, slots, tiles)
            cross = nt_dot(pool[index], doubled)
            level = jnp.minimum(cross + (norm_b[index] + own_norm), 0.0)
            value = jnp.exp(level / (band_b[index] + own_band))
            if slot >= NEAR - 1:
                value = jnp.where(slot < live, value, 0.0)
            kernel_half[tile, slot] = value.astype(jnp.bfloat16)
            total = total + jnp.sum(value.reshape(size // 8, 8, size), axis=0)
        inverse[tile] = 1.0 / jnp.sum(total, axis=0, keepdims=True)
        return carry

    lax.fori_loop(0, tiles, one_tile, 0)


def build_kernel(table, counts, pool, band, tiles, slots):
    count, size, _ = pool.shape
    return pl.pallas_call(
        functools.partial(kernel_body, tiles, slots),
        out_shape=(
            jax.ShapeDtypeStruct((tiles, slots, size, size), jnp.bfloat16),
            jax.ShapeDtypeStruct((tiles, 1, size), jnp.float32),
        ),
        in_specs=[SMEM, SMEM, VMEM, VMEM],
        out_specs=(VMEM, VMEM),
        scratch_shapes=[
            pltpu.VMEM((count, size, size), jnp.float32),
            pltpu.VMEM((count, size, size), jnp.float32),
            pltpu.VMEM((tiles, 1, size), jnp.float32),
        ],
        name="kernel_density",
    )(table, counts, pool, band)


def walk_body(
    tiles, slots, table, pool, prior, inverse, projection, kernel_half, raw, degree, gram, scaled
):
    size = pool.shape[1]
    columns = projection.shape[0]

    def prepare(index, carry):
        start = nt_dot(projection[...], pool[index])
        inv = inverse[index]
        scaled[index, 0:columns, :] = (start * (prior[index] * inv)).astype(jnp.bfloat16)
        high = inv.astype(jnp.bfloat16).astype(jnp.float32)
        row = lax.broadcasted_iota(jnp.int32, (16, size), 0)
        extra = jnp.where(row == 0, high, jnp.where(row == 1, inv - high, 0.0))
        scaled[index, columns : columns + 16, :] = extra.astype(jnp.bfloat16)
        return carry

    lax.fori_loop(0, pool.shape[0], prepare, 0)
    gram[...] = jnp.zeros_like(gram)

    def one_tile(tile, carry):
        total = jnp.zeros((columns + 16, size), jnp.float32)
        for slot in range(slots):
            index = slot_tile(table, tile, slot, slots, tiles)
            total = total + jnp.dot(
                scaled[index], kernel_half[tile, slot], preferred_element_type=jnp.float32
            )
        below = total[columns : columns + 1] + total[columns + 1 : columns + 2]
        degree[tile] = below
        value = total[0:columns] / below
        raw[:, pl.ds(pl.multiple_of(tile * size, size), size)] = value
        gram[...] += nt_dot(value, value, lax.Precision.HIGHEST)
        return carry

    lax.fori_loop(0, tiles, one_tile, 0)


def first_walk(table, pool, prior, inverse, projection, kernel_half):
    tiles, slots, size, _ = kernel_half.shape
    columns = projection.shape[0]
    return pl.pallas_call(
        functools.partial(walk_body, tiles, slots),
        out_shape=(
            jax.ShapeDtypeStruct((columns, tiles * size), jnp.float32),
            jax.ShapeDtypeStruct((tiles, 1, size), jnp.float32),
            jax.ShapeDtypeStruct((columns, columns), jnp.float32),
        ),
        in_specs=[SMEM, VMEM, VMEM, VMEM, VMEM, VMEM],
        out_specs=(VMEM, VMEM, VMEM),
        scratch_shapes=[pltpu.VMEM((pool.shape[0], columns + 16, size), jnp.bfloat16)],
        name="first_walk",
    )(table, pool, prior, inverse, projection, kernel_half)


def basis_body(tiles, lower_inverse, raw, inverse, basis, scaled):
    size = inverse.shape[2]
    value = jnp.dot(
        lower_inverse[...],
        raw[...],
        precision=lax.Precision.HIGHEST,
        preferred_element_type=jnp.float32,
    )
    basis[...] = value
    for tile in range(tiles):
        part = value[:, tile * size : (tile + 1) * size]
        scaled[tile] = (part * inverse[tile]).astype(jnp.bfloat16)


def first_basis_of(lower_inverse, raw, inverse):
    tiles, _, size = inverse.shape
    columns = raw.shape[0]
    return pl.pallas_call(
        functools.partial(basis_body, tiles),
        out_shape=(
            jax.ShapeDtypeStruct(raw.shape, jnp.float32),
            jax.ShapeDtypeStruct((tiles, columns, size), jnp.bfloat16),
        ),
        in_specs=[VMEM, VMEM, VMEM],
        out_specs=(VMEM, VMEM),
        name="first_basis",
    )(lower_inverse, raw, inverse)


def apply_body(tiles, slots, table, own, far, degree, kernel_half, raw, gram):
    size = own.shape[2]
    columns = own.shape[1]
    gram[...] = jnp.zeros_like(gram)

    def one_tile(tile, carry):
        total = jnp.zeros((columns, size), jnp.float32)
        for slot in range(slots):
            if slot < NEAR:
                left = own[table[tile * slots + slot]]
            else:
                left = far[tile * (slots - NEAR) + (slot - NEAR)]
            total = total + jnp.dot(
                left, kernel_half[tile, slot], preferred_element_type=jnp.float32
            )
        value = total / degree[tile]
        raw[:, pl.ds(pl.multiple_of(tile * size, size), size)] = value
        gram[...] += nt_dot(value, value, lax.Precision.HIGHEST)
        return carry

    lax.fori_loop(0, tiles, one_tile, 0)


def second_walk(table, own, far, degree, kernel_half):
    tiles, slots, size, _ = kernel_half.shape
    columns = own.shape[1]
    return pl.pallas_call(
        functools.partial(apply_body, tiles, slots),
        out_shape=(
            jax.ShapeDtypeStruct((columns, tiles * size), jnp.float32),
            jax.ShapeDtypeStruct((columns, columns), jnp.float32),
        ),
        in_specs=[SMEM, VMEM, VMEM, VMEM, VMEM],
        out_specs=(VMEM, VMEM),
        name="second_walk",
    )(table, own, far, degree, kernel_half)


def reduce_body(nz, ny, local, out, parts_w, parts_y, parts_z, stage, sw, rw, sy, ry, sz, rz, sa, ra):
    row = lax.axis_index("rows")
    y = lax.axis_index("grp")
    w = row % PLANE
    z = row // PLANE

    def peer_w(step):
        other = (w + step) % PLANE
        return other, (z * PLANE + other, y)

    def peer_y(step):
        other = (y + step) % ny
        return other, (row, other)

    def peer_z(step):
        other = (z + step) % nz
        return other, (other * PLANE + w, y)

    barrier = pltpu.get_barrier_semaphore()
    for count, peer in ((PLANE, peer_w), (ny, peer_y), (nz, peer_z)):

        def greet(step, carry):
            pl.semaphore_signal(barrier, inc=1, device_id=peer(step)[1], device_id_type=MESH)
            return carry

        lax.fori_loop(1, count, greet, 0)
    pl.semaphore_wait(barrier, PLANE + ny + nz - 3)

    def exchange(count, peer, me, source, target, send, recv):
        def copy(step, mine):
            other, device = peer(step)
            return pltpu.make_async_remote_copy(
                src_ref=source(other),
                dst_ref=target.at[me if mine else other],
                send_sem=send.at[other],
                recv_sem=recv.at[me if mine else other],
                device_id=device,
                device_id_type=MESH,
            )

        def start(step, carry):
            copy(step, True).start()
            return carry

        def finish(step, carry):
            copy(step, True).wait_send()
            copy(step, False).wait_recv()
            return carry

        lax.fori_loop(1, count, start, 0)
        lax.fori_loop(1, count, finish, 0)

    exchange(PLANE, peer_w, w, lambda other: local.at[other], parts_w, sw, rw)
    parts_w[w] = local[w]
    stage[0] = jnp.sum(parts_w[...], axis=0)
    exchange(ny, peer_y, y, lambda other: stage.at[0], parts_y, sy, ry)
    parts_y[y] = stage[0]
    stage[1] = jnp.sum(parts_y[...], axis=0)
    exchange(nz, peer_z, z, lambda other: stage.at[1], parts_z, sz, rz)
    parts_z[z] = stage[1]
    stage[2] = jnp.sum(parts_z[...], axis=0)
    exchange(PLANE, peer_w, w, lambda other: stage.at[2], out, sa, ra)
    out[w] = stage[2]


def total_gram(gram):
    columns = gram.shape[0]
    height = columns // PLANE
    ny = lax.axis_size("grp")
    nz = lax.axis_size("rows") // PLANE
    chunk = (height, columns)
    dma = pltpu.SemaphoreType.DMA
    out = pl.pallas_call(
        functools.partial(reduce_body, nz, ny),
        out_shape=jax.ShapeDtypeStruct((PLANE,) + chunk, jnp.float32),
        in_specs=[VMEM],
        out_specs=VMEM,
        scratch_shapes=[
            pltpu.VMEM((PLANE,) + chunk, jnp.float32),
            pltpu.VMEM((ny,) + chunk, jnp.float32),
            pltpu.VMEM((nz,) + chunk, jnp.float32),
            pltpu.VMEM((3,) + chunk, jnp.float32),
            dma((PLANE,)),
            dma((PLANE,)),
            dma((ny,)),
            dma((ny,)),
            dma((nz,)),
            dma((nz,)),
            dma((PLANE,)),
            dma((PLANE,)),
        ],
        compiler_params=pltpu.CompilerParams(collective_id=0, has_side_effects=True),
        name="gram_reduce",
    )(gram.reshape((PLANE,) + chunk))
    return out.reshape(columns, columns)


def lower_inverse_of(gram, total_rows):
    lower = jnp.linalg.cholesky(total_gram(gram) / total_rows)
    identity = jnp.eye(gram.shape[0], dtype=jnp.float32)
    return lax.linalg.triangular_solve(lower, identity, left_side=True, lower=True)


def exchange_tiles(tiles, requested, owner):
    sent = jnp.take(tiles, requested, axis=0, mode="clip")
    got = lax.all_to_all(sent, "rows", split_axis=0, concat_axis=0, tiled=True)
    return jnp.take(got, owner, axis=0, mode="clip")


def shards(features, length_scale, prior, partners, counts, projection):
    tiles, slots = partners.shape[1:]
    size = features.shape[1] // tiles
    columns = projection.shape[1]
    nrows = lax.axis_size("rows")
    device_index = lax.axis_index("rows")
    own_rows = features[0].reshape(tiles, size, features.shape[2])
    own_side = jnp.stack(
        [length_scale[0].reshape(tiles, size), prior[0].reshape(tiles, size)], axis=1
    )
    lists = partners[0]
    far_tiles = lists[:, NEAR:].reshape(-1)
    owner = far_tiles // tiles
    hits = owner[:, None] == jnp.arange(nrows, dtype=jnp.int32)[None, :]
    wanted = jnp.sum(jnp.where(hits, (far_tiles % tiles)[:, None], 0), axis=0)
    requested = lax.all_to_all(wanted, "rows", split_axis=0, concat_axis=0, tiled=True)
    table = (lists - device_index * tiles).reshape(-1)

    far_side = exchange_tiles(own_side, requested, owner)
    far_rows = exchange_tiles(own_rows, requested, owner)
    pool = jnp.concatenate([own_rows, far_rows], axis=0)
    side = jnp.concatenate([own_side, far_side], axis=0).astype(jnp.float32)
    band = side[:, 0:1, :]
    prior_rows = side[:, 1:2, :]
    kernel_half, own_inverse = build_kernel(table, counts[0], pool, band, tiles, slots)
    far_inverse = exchange_tiles(own_inverse.astype(jnp.bfloat16), requested, owner)
    inverse = jnp.concatenate([own_inverse, far_inverse.astype(jnp.float32)], axis=0)
    raw, degree, gram = first_walk(
        table, pool, prior_rows, inverse, projection.T, kernel_half
    )
    total_rows = nrows * lax.axis_size("grp") * tiles * size
    basis, own_next = first_basis_of(lower_inverse_of(gram, total_rows), raw, own_inverse)
    far_next = exchange_tiles(own_next, requested, owner)
    second_raw, second_gram = second_walk(table, own_next, far_next, degree, kernel_half)
    embedding = jnp.dot(
        lower_inverse_of(second_gram, total_rows), second_raw, precision=lax.Precision.HIGHEST
    )
    return basis[None], embedding[None]


def solution(mesh):
    in_specs = (
        P("grp", "rows", None),
        P("grp", "rows"),
        P("grp", "rows"),
        P("grp", "rows", None),
        P("grp", "rows"),
        P(),
    )
    out_specs = (P("grp", None, "rows"), P("grp", None, "rows"))
    return jax.shard_map(shards, mesh=mesh, in_specs=in_specs, out_specs=out_specs, check_vma=False)
```

time: 850 us -> 533 us (0.63); the launches traced: 839 us -> 532 us
  waiting for transfers between devices: 326 us -> 208 us
  local copies, waits for them, and re-layouts: 133 us -> 17.7 us
  Pallas kernels: 0 us -> 105 us
  blocking collectives: 202 us -> 130 us
  matrix products: 40 us -> 3.32 us
  starting transfers between devices: 63.9 us -> 32.8 us
  other arithmetic: 60.4 us -> 33.9 us
  loops' own time: 11.9 us -> 0 us
    psum x2 -> x0, blocking collectives: 202 us -> none  [orthonormal(): gram_matrix = lax.psum(local_gram, ('rows', 'grp')) / total_rows]
    all_to_all x0 -> x2, blocking collectives: none -> 130 us  [exchange_tiles(): got = lax.all_to_all(sent, 'rows', split_axis=0, concat_axis=0, tiled=True)]
    all_to_all x5 -> x2, waiting for transfers between devices: 313 us -> 193 us  [exchange_tiles(): got = lax.all_to_all(sent, 'rows', split_axis=0, concat_axis=0, tiled=True)]
    pallas_call x0 -> x6, Pallas kernels: none -> 105 us  [the longest x2 56.3 us: total_gram(): pl.pallas_call(functools.partial(reduce_body, nz, ny), out_shape=jax.Shap...]
    gather x77 -> x9, local copies, waits for them, and re-layouts: 113 us -> 14.3 us  [the longest x4 7.28 us: exchange_tiles(): return jnp.take(got, owner, axis=0, mode='clip')]
    dot_general x30 -> x1, matrix products: 39.5 us -> 2.21 us  [shards(): jnp.dot(lower_inverse_of(second_gram, total_rows), second_raw, precision=...]
    all_to_all x5 -> x2, starting transfers between devices: 43.5 us -> 12.4 us  [exchange_tiles(): got = lax.all_to_all(sent, 'rows', split_axis=0, concat_axis=0, tiled=True)]
    another operation x3 -> x0, loops' own time: 11.9 us -> none  [sweep_blocks(): lax.map(one_block, jnp.arange(tiles_dev // block_size, dtype=jnp.int32))]
  transfers between devices with their start and end apart: 6 -> 3, of which waited for: 6 -> 3; matrix products, arithmetic and copies ran while one was open for 2% -> 1% of each run, Pallas kernels for 0% -> 0%
where the time goes in v1:
time: 533 us; the launch traced here: 532 us
  waiting for transfers between devices  208 us (39%)
  blocking collectives  130 us (24%)
  Pallas kernels  105 us (20%)
  other arithmetic  33.9 us (6%)
  starting transfers between devices  32.8 us (6%)
  local copies, waits for them, and re-layouts  17.7 us (3%)
    all_to_all x2, waiting for transfers between devices, exchange_tiles(): got = lax.all_to_all(sent, 'rows', split_axis=0, concat_axis=0, tiled=True)  193 us
    all_to_all x2, blocking collectives, exchange_tiles(): got = lax.all_to_all(sent, 'rows', split_axis=0, concat_axis=0, tiled=True)  130 us
    pallas_call x2, Pallas kernels, total_gram(): pl.pallas_call(functools.partial(reduce_body, nz, ny), out_shape=jax.Shap...  56.3 us
    all_to_all x1, starting transfers between devices, shards(): lax.all_to_all(wanted, 'rows', split_axis=0, concat_axis=0, tiled=True)  20.4 us
    pallas_call x1, Pallas kernels, first_walk(): pl.pallas_call(functools.partial(walk_body, tiles, slots), out_shape=(jax...  18.6 us
    pallas_call x1, Pallas kernels, build_kernel(): pl.pallas_call(functools.partial(kernel_body, tiles, slots), out_shape=(j...  18 us
    all_to_all x1, waiting for transfers between devices, shards(): lax.all_to_all(wanted, 'rows', split_axis=0, concat_axis=0, tiled=True)  14.1 us
    another operation x6, other arithmetic, lower_inverse_of(): lower = jnp.linalg.cholesky(total_gram(gram) / total_rows)  13 us
  transfers between devices with their start and end apart: 3, of which 3 were waited for; matrix products, arithmetic and copies ran while one was open for 1% of the time, Pallas kernels for 0%

profile of v1, /device:TPU:1, one launch (start us, length us, event | category | flops | bytes accessed | tf_op | source)
XLA Modules:
  0.0 531.8 jit_solution(8630282513590926895)
XLA Ops:
  0.6 0.7 copy.32
  1.6 0.1 ne.56
  1.8 0.1 select_reduce_fusion.2
  1.9 0.7 copy.21
  2.7 20.4 %all-to-all-start = ((s32[128,1,1]{2,1,0:T(1,128)}), s32[128,1,1]{2,1,0:T(1,128)S(1)}, u32[]{:S(2)}, u32[]{:S(2)}) async-start(s32[128,1,1]{2,1,0:T(1,128)} %copy.21), calls=%async_computation | async-start | bytes 131072 | tf_op jit(solution)/shard_map/all_to_all | solution.py:335
  23.1 0.7 pad_maximum_fusion.2
  23.8 14.1 %all-to-all-done = s32[128,1,1]{2,1,0:T(1,128)S(1)} async-done(((s32[128,1,1]{2,1,0:T(1,128)}), s32[128,1,1]{2,1,0:T(1,128)S(1)}, u32[]{:S(2)}, u32[]{:S(2)}) %all-to-all-start) | async-done | bytes 544 | tf_op jit(solution)/shard_map/all_to_all | solution.py:335
  37.9 2.3 reduce.5
  40.3 1.4 gather_fusion.2
  41.6 5.6 %all-to-all-start.2 = ((bf16[128,2,128]{2,1,0:T(2,128)(2,1)}), bf16[128,2,128]{2,1,0:T(2,128)(2,1)S(1)}, u32[]{:S(2)}, u32[]{:S(2)}) async-start(bf16[128,2,128]{2,1,0:T(2,128)(2,1)} %gather_fusion.2), calls=%async_computation.2 | async-start | bytes 131072 | tf_op jit(solution)/shard_map/all_to_all | solution.py:316
  47.3 3.1 gather_fusion
  50.4 12.0 %all-to-all-done.2 = bf16[128,2,128]{2,1,0:T(2,128)(2,1)S(1)} async-done(((bf16[128,2,128]{2,1,0:T(2,128)(2,1)}), bf16[128,2,128]{2,1,0:T(2,128)(2,1)S(1)}, u32[]{:S(2)}, u32[]{:S(2)}) %all-to-all-start.2) | async-done | bytes 65568 | tf_op jit(solution)/shard_map/all_to_all | solution.py:316
  62.3 6.7 %all-to-all-start.1 = ((bf16[128,128,128]{2,1,0:T(8,128)(2,1)}), bf16[128,128,128]{2,1,0:T(8,128)(2,1)}, u32[]{:S(2)}, u32[]{:S(2)}) async-start(bf16[128,128,128]{2,1,0:T(8,128)(2,1)} %gather_fusion), calls=%async_computation.1 | async-start | bytes 8388608 | tf_op jit(solution)/shard_map/all_to_all | solution.py:316
  69.2 0.6 sub.20.table
  69.9 0.6 gather_fusion.3
  70.6 0.6 fusion.11
  71.2 181.5 %all-to-all-done.1 = bf16[128,128,128]{2,1,0:T(8,128)(2,1)} async-done(((bf16[128,128,128]{2,1,0:T(8,128)(2,1)}), bf16[128,128,128]{2,1,0:T(8,128)(2,1)}, u32[]{:S(2)}, u32[]{:S(2)}) %all-to-all-start.1) | async-done | bytes 4194336 | tf_op jit(solution)/shard_map/all_to_all | solution.py:316
  252.7 3.0 gather_fusion.1
  255.7 1.3 pad_maximum_fusion.pool
  257.0 18.0 %kernel_density.1 = (bf16[12,16,128,128]{3,2,1,0:T(8,128)(2,1)}, f32[12,1,128]{2,1,0:T(1,128)}) custom-call(s32[192]{0:T(256)} %sub.20.table, s32[12]{0:T(128)} %bitcast.65, bf16[48,128,128]{2,1,0:T(8,128)(2,1)} %pad_maximum_fusion.pool, f32[48,1,128]{2,1,0:T(1,128)} %get-tuple-element.24.band), custom_call_target="tpu_custom_call" | custom-call | tf_op jit(solution)/shard_map/kernel_density/pallas_call | solution.py:74
  274.9 0.7 convert_element_type.24
  275.6 0.7 gather_fusion.4
  276.4 27.8 %all_to_all.29 = bf16[128,1,128]{2,1,0:T(2,128)(2,1)S(1)} all-to-all(bf16[128,1,128]{2,1,0:T(2,128)(2,1)S(1)} %copy.22), channel_id=1, replica_groups=mesh['rows'=128,'grp'=4] {'rows'}, dimensions={0} | all-to-all | bytes 65536 | tf_op jit(solution)/shard_map/all_to_all | solution.py:316
  304.2 0.6 gather_fusion.5
  304.8 1.3 pad_maximum_fusion.1.inverse
  306.1 18.6 %first_walk.1 = (f32[64,1536]{1,0:T(8,128)}, f32[12,1,128]{2,1,0:T(1,128)}, f32[64,64]{1,0:T(8,128)}) custom-call(s32[192]{0:T(256)} %sub.20.table, bf16[48,128,128]{2,1,0:T(8,128)(2,1)} %pad_maximum_fusion.pool, f32[48,1,128]{2,1,0:T(1,128)} %get-tuple-element.25.prior, f32[48,1,128]{2,1,0:T(1,128)} %pad_maximum_fusion.1.inverse, bf16[64,128]{1,0:T(8,128)(2,1)} %bitcast.64, ...), custom_call_target="tpu_custom_call" | custom-call | tf_op jit(solution)/shard_map/first_walk/pallas_call | solution.py:130
  324.7 27.8 %gram_reduce.2 = f32[8,8,64]{2,1,0:T(8,128)} custom-call(f32[8,8,64]{2,1,0:T(8,128)} %bitcast.59), custom_call_target="tpu_custom_call" | custom-call | tf_op jit(solution)/shard_map/gram_reduce/pallas_call | solution.py:283
  352.5 0.8 multiply_bitcast_fusion.1
  353.3 0.8 fusion.9
  354.1 5.8 %cholesky.44 = f32[64,64]{1,0:T(8,128)S(1)} custom-call(f32[64,64]{1,0:T(8,128)S(1)} %fusion.9), custom_call_target="Cholesky" | custom-call | tf_op jit(solution)/shard_map/jit(cholesky)/cholesky | solution.py:309
  360.0 0.6 compare_reduce_fusion.1
  360.6 0.7 fusion.4
  361.3 4.9 custom-call.6
  366.2 0.9 fusion.2.lower_inverse
  367.0 2.3 first_basis.1
  369.3 1.9 gather_fusion.6
  371.2 102.5 %all_to_all.30 = bf16[128,64,128]{2,1,0:T(8,128)(2,1)} all-to-all(bf16[128,64,128]{2,1,0:T(8,128)(2,1)S(1)} %gather_fusion.6), channel_id=1, replica_groups=mesh['rows'=128,'grp'=4] {'rows'}, dimensions={0} | all-to-all | bytes 4194304 | tf_op jit(solution)/shard_map/all_to_all | solution.py:316
  473.7 3.1 gather_fusion.7
  476.8 10.3 %second_walk.1 = (f32[64,1536]{1,0:T(8,128)}, f32[64,64]{1,0:T(8,128)}) custom-call(s32[192]{0:T(256)} %sub.20.table, bf16[12,64,128]{2,1,0:T(8,128)(2,1)} %get-tuple-element.18.own, bf16[36,64,128]{2,1,0:T(8,128)(2,1)} %gather_fusion.7, f32[12,1,128]{2,1,0:T(1,128)} %get-tuple-element.19.degree, bf16[12,16,128,128]{3,2,1,0:T(8,128)(2,1)} %get-tuple-element.14.kernel_half), custom_call_target="tpu_custom_call" | custom-call | tf_op jit(solution)/shard_map/second_walk/pallas_call | solution.py:199
  487.1 28.5 %gram_reduce.3 = f32[8,8,64]{2,1,0:T(8,128)} custom-call(f32[8,8,64]{2,1,0:T(8,128)} %bitcast.58), custom_call_target="tpu_custom_call" | custom-call | tf_op jit(solution)/shard_map/gram_reduce/pallas_call | solution.py:283
  515.6 0.8 multiply_bitcast_fusion
  516.4 0.8 fusion.7
  517.2 5.8 %cholesky.55 = f32[64,64]{1,0:T(8,128)S(1)} custom-call(f32[64,64]{1,0:T(8,128)S(1)} %fusion.7), custom_call_target="Cholesky" | custom-call | tf_op jit(solution)/shard_map/jit(cholesky)/cholesky | solution.py:309
  523.1 0.6 compare_reduce_fusion
  523.7 0.7 fusion.5
  524.4 4.9 custom-call.7
  529.3 0.3 fusion
  529.6 2.2 convolution_bitcast_fusion
  (28 shorter events, 0.9 us)
Async XLA Ops:
  0.6 46.7 %copy-start = (bf16[1,1536,128]{2,1,0:T(8,128)(2,1)S(1)}, bf16[1,1536,128]{2,1,0:T(8,128)(2,1)}, u32[]{:S(2)}) copy-start(bf16[1,1536,128]{2,1,0:T(8,128)(2,1)} %param.9) | copy-start | bytes 1179652
  2.7 35.2 %all-to-all-start = ((s32[128,1,1]{2,1,0:T(1,128)}), s32[128,1,1]{2,1,0:T(1,128)S(1)}, u32[]{:S(2)}, u32[]{:S(2)}) async-start(s32[128,1,1]{2,1,0:T(1,128)} %copy.21), calls=%async_computation | async-start | bytes 131072 | tf_op jit(solution)/shard_map/all_to_all | solution.py:335
  41.6 20.7 %all-to-all-start.2 = ((bf16[128,2,128]{2,1,0:T(2,128)(2,1)}), bf16[128,2,128]{2,1,0:T(2,128)(2,1)S(1)}, u32[]{:S(2)}, u32[]{:S(2)}) async-start(bf16[128,2,128]{2,1,0:T(2,128)(2,1)} %gather_fusion.2), calls=%async_computation.2 | async-start | bytes 131072 | tf_op jit(solution)/shard_map/all_to_all | solution.py:316
  50.3 18.8 %copy-start.1 = (s32[1,12,16]{2,0,1:T(1,128)S(1)}, s32[1,12,16]{2,0,1:T(1,128)}, u32[]{:S(2)}) copy-start(s32[1,12,16]{2,0,1:T(1,128)} %param.12) | copy-start | bytes 2308
  50.3 20.2 %copy-start.2 = (bf16[1,1536]{1,0:T(2,128)(2,1)S(1)}, bf16[1,1536]{1,0:T(2,128)(2,1)}, u32[]{:S(2)}) copy-start(bf16[1,1536]{1,0:T(2,128)(2,1)} %param.11) | copy-start | bytes 9220
  50.3 20.2 %copy-start.3 = (bf16[1,1536]{1,0:T(2,128)(2,1)S(1)}, bf16[1,1536]{1,0:T(2,128)(2,1)}, u32[]{:S(2)}) copy-start(bf16[1,1536]{1,0:T(2,128)(2,1)} %param.10) | copy-start | bytes 9220
  62.3 190.4 %all-to-all-start.1 = ((bf16[128,128,128]{2,1,0:T(8,128)(2,1)}), bf16[128,128,128]{2,1,0:T(8,128)(2,1)}, u32[]{:S(2)}, u32[]{:S(2)}) async-start(bf16[128,128,128]{2,1,0:T(8,128)(2,1)} %gather_fusion), calls=%async_computation.1 | async-start | bytes 8388608 | tf_op jit(solution)/shard_map/all_to_all | solution.py:316

commit v2 on v1

v2 whole, which is shorter than its diff:
```python
import functools

import jax
import jax.numpy as jnp
from jax import lax
from jax.experimental import pallas as pl
from jax.experimental.pallas import tpu as pltpu
from jax.sharding import PartitionSpec as P

NEAR = 13
PLANE = 8
MESH = pl.DeviceIdType.MESH
VMEM = pl.BlockSpec(memory_space=pltpu.VMEM)
SMEM = pl.BlockSpec(memory_space=pltpu.SMEM)


def nt_dot(left, right, precision=None):
    return lax.dot_general(
        left,
        right,
        (((1,), (1,)), ((), ())),
        precision=precision,
        preferred_element_type=jnp.float32,
    )


def load_norm(rows):
    wide = rows.astype(jnp.float32)
    norm = jnp.sum(wide * wide, axis=1, keepdims=True)
    return jnp.broadcast_to(-norm, (rows.shape[0], rows.shape[0]))


def column_band(row):
    return jnp.transpose(jnp.broadcast_to(row, (row.shape[1], row.shape[1])))


def kernel_value(rows, norm, band, doubled, own_norm, own_band):
    level = jnp.minimum(nt_dot(rows, doubled) + (norm + own_norm), 0.0)
    return jnp.exp(level / (band + own_band))


def fold_rows(value):
    return jnp.sum(value.reshape(value.shape[0] // 8, 8, value.shape[1]), axis=0)


def near_kernel_body(
    tiles, slots, table, counts, pool, band, kernel_half, density, norm_a, norm_b, band_b
):
    size = pool.shape[1]

    def prepare(index, carry):
        wide = load_norm(pool[index])
        norm_b[index] = wide
        band_b[index] = column_band(band[index])
        norm_a[index] = jnp.transpose(wide)[0:1, :]
        return carry

    lax.fori_loop(0, tiles, prepare, 0)

    def one_tile(tile, carry):
        doubled = pool[tile] * jnp.bfloat16(2)
        own_norm = norm_a[tile]
        own_band = band[tile]
        live = counts[tile]
        total = jnp.zeros((8, size), jnp.float32)
        for slot in range(NEAR):
            index = table[tile * slots + slot]
            value = kernel_value(
                pool[index], norm_b[index], band_b[index], doubled, own_norm, own_band
            )
            if slot == NEAR - 1:
                value = jnp.where(slot < live, value, 0.0)
            kernel_half[tile, slot] = value.astype(jnp.bfloat16)
            total = total + fold_rows(value)
        density[tile] = jnp.sum(total, axis=0, keepdims=True)
        return carry

    lax.fori_loop(0, tiles, one_tile, 0)


def near_kernel(table, counts, pool, band, slots):
    tiles, size, _ = pool.shape
    return pl.pallas_call(
        functools.partial(near_kernel_body, tiles, slots),
        out_shape=(
            jax.ShapeDtypeStruct((tiles, NEAR, size, size), jnp.bfloat16),
            jax.ShapeDtypeStruct((tiles, 1, size), jnp.float32),
            jax.ShapeDtypeStruct((tiles, 1, size), jnp.float32),
        ),
        in_specs=[SMEM, SMEM, VMEM, VMEM],
        out_specs=(VMEM, VMEM, VMEM),
        scratch_shapes=[pltpu.VMEM((tiles, size, size), jnp.float32)] * 2,
        cost_estimate=cost(tiles * NEAR * size * size, 400),
        name="near_kernel",
    )(table, counts, pool, band)


def far_kernel_body(tiles, slots, counts, pool, band, far, far_band, norm_a, near, kernel_half, inverse):
    far_slots = slots - NEAR

    def one_tile(tile, carry):
        doubled = pool[tile] * jnp.bfloat16(2)
        live = counts[tile]
        total = jnp.zeros((8, pool.shape[1]), jnp.float32)
        for slot in range(far_slots):
            index = tile * far_slots + slot
            rows = far[index]
            value = kernel_value(
                rows,
                load_norm(rows),
                column_band(far_band[index]),
                doubled,
                norm_a[tile],
                band[tile],
            )
            value = jnp.where(slot + NEAR < live, value, 0.0)
            kernel_half[tile, slot] = value.astype(jnp.bfloat16)
            total = total + fold_rows(value)
        inverse[tile] = 1.0 / (near[tile] + jnp.sum(total, axis=0, keepdims=True))
        return carry

    lax.fori_loop(0, tiles, one_tile, 0, unroll=2)


def far_kernel(counts, pool, band, far, far_band, norm_a, near, slots):
    tiles, size, _ = pool.shape
    return pl.pallas_call(
        functools.partial(far_kernel_body, tiles, slots),
        out_shape=(
            jax.ShapeDtypeStruct((tiles, slots - NEAR, size, size), jnp.bfloat16),
            jax.ShapeDtypeStruct((tiles, 1, size), jnp.float32),
        ),
        in_specs=[SMEM] + [VMEM] * 6,
        out_specs=(VMEM, VMEM),
        name="far_kernel",
    )(counts, pool, band, far, far_band, norm_a, near)


def cost(flops, scale):
    return pl.CostEstimate(flops=flops * scale, bytes_accessed=flops * 4, transcendentals=flops)


def scale_start(projection, rows, prior, inv):
    start = nt_dot(projection, rows)
    scaled = (start * (prior * inv)).astype(jnp.bfloat16)
    high = inv.astype(jnp.bfloat16).astype(jnp.float32)
    row = lax.broadcasted_iota(jnp.int32, (16, inv.shape[1]), 0)
    extra = jnp.where(row == 0, high, jnp.where(row == 1, inv - high, 0.0))
    return scaled, extra.astype(jnp.bfloat16)


def near_walk_body(
    tiles, slots, table, pool, prior, inverse, projection, kernel_half, partial, scaled
):
    columns = projection.shape[0]

    def prepare(index, carry):
        main, extra = scale_start(projection[...], pool[index], prior[index], inverse[index])
        scaled[index, 0:columns, :] = main
        scaled[index, columns : columns + 16, :] = extra
        return carry

    lax.fori_loop(0, tiles, prepare, 0, unroll=2)

    def one_tile(tile, carry):
        total = jnp.zeros(partial.shape[1:], jnp.float32)
        for slot in range(NEAR):
            total = total + jnp.dot(
                scaled[table[tile * slots + slot]],
                kernel_half[tile, slot],
                preferred_element_type=jnp.float32,
            )
        partial[tile] = total
        return carry

    lax.fori_loop(0, tiles, one_tile, 0)


def near_walk(table, pool, prior, inverse, projection, kernel_half, slots):
    tiles, _, size, _ = kernel_half.shape
    height = projection.shape[0] + 16
    return pl.pallas_call(
        functools.partial(near_walk_body, tiles, slots),
        out_shape=jax.ShapeDtypeStruct((tiles, height, size), jnp.float32),
        in_specs=[SMEM] + [VMEM] * 5,
        out_specs=VMEM,
        scratch_shapes=[pltpu.VMEM((tiles, height, size), jnp.bfloat16)],
        cost_estimate=cost(tiles * NEAR * size * size, 160),
        name="near_walk",
    )(table, pool, prior, inverse, projection, kernel_half)


def far_walk_body(
    tiles, far, prior, inverse, projection, kernel_half, partial, raw, half, degree, gram, scaled
):
    size = far.shape[1]
    columns = projection.shape[0]
    far_slots = kernel_half.shape[1]
    gram[...] = jnp.zeros_like(gram)

    def prepare(index, carry):
        main, extra = scale_start(projection[...], far[index], prior[index], inverse[index])
        scaled[index, 0:columns, :] = main
        scaled[index, columns : columns + 16, :] = extra
        return carry

    lax.fori_loop(0, far.shape[0], prepare, 0, unroll=4)

    def one_tile(tile, carry):
        total = partial[tile]
        for slot in range(far_slots):
            total = total + jnp.dot(
                scaled[tile * far_slots + slot],
                kernel_half[tile, slot],
                preferred_element_type=jnp.float32,
            )
        below = total[columns : columns + 1] + total[columns + 1 : columns + 2]
        degree[tile] = below
        value = total[0:columns] / below
        raw[:, pl.ds(pl.multiple_of(tile * size, size), size)] = value
        half[tile] = value.astype(jnp.bfloat16)
        return carry

    lax.fori_loop(0, tiles, one_tile, 0, unroll=2)
    gram[...] = nt_dot(raw[...], raw[...], lax.Precision.HIGHEST)


def far_walk(far, prior, inverse, projection, kernel_half, partial):
    tiles, _, size, _ = kernel_half.shape
    columns = projection.shape[0]
    return pl.pallas_call(
        functools.partial(far_walk_body, tiles),
        out_shape=(
            jax.ShapeDtypeStruct((columns, tiles * size), jnp.float32),
            jax.ShapeDtypeStruct((tiles, columns, size), jnp.bfloat16),
            jax.ShapeDtypeStruct((tiles, 1, size), jnp.float32),
            jax.ShapeDtypeStruct((columns, columns), jnp.float32),
        ),
        in_specs=[VMEM] * 6,
        out_specs=(VMEM,) * 4,
        scratch_shapes=[pltpu.VMEM((far.shape[0], columns + 16, size), jnp.bfloat16)],
        name="far_walk",
    )(far, prior, inverse, projection, kernel_half, partial)


def near_apply_body(
    tiles, slots, table, lower_inverse, raw, inverse, kernel_half, basis, partial, scaled
):
    size = inverse.shape[2]
    value = jnp.dot(
        lower_inverse[...],
        raw[...],
        precision=lax.Precision.HIGHEST,
        preferred_element_type=jnp.float32,
    )
    basis[...] = value
    for tile in range(tiles):
        part = value[:, tile * size : (tile + 1) * size]
        scaled[tile] = (part * inverse[tile]).astype(jnp.bfloat16)

    def one_tile(tile, carry):
        total = jnp.zeros(partial.shape[1:], jnp.float32)
        for slot in range(NEAR):
            total = total + jnp.dot(
                scaled[table[tile * slots + slot]],
                kernel_half[tile, slot],
                preferred_element_type=jnp.float32,
            )
        partial[tile] = total
        return carry

    lax.fori_loop(0, tiles, one_tile, 0)


def near_apply(table, lower_inverse, raw, inverse, kernel_half, slots):
    tiles, _, size, _ = kernel_half.shape
    columns = raw.shape[0]
    return pl.pallas_call(
        functools.partial(near_apply_body, tiles, slots),
        out_shape=(
            jax.ShapeDtypeStruct(raw.shape, jnp.float32),
            jax.ShapeDtypeStruct((tiles, columns, size), jnp.float32),
        ),
        in_specs=[SMEM] + [VMEM] * 4,
        out_specs=(VMEM, VMEM),
        scratch_shapes=[pltpu.VMEM((tiles, columns, size), jnp.bfloat16)],
        cost_estimate=cost(tiles * NEAR * size * size, 128),
        name="near_apply",
    )(table, lower_inverse, raw, inverse, kernel_half)


def far_apply_body(tiles, lower_inverse, far, inverse, degree, kernel_half, partial, raw, gram, scaled):
    size = far.shape[2]
    far_slots = kernel_half.shape[1]

    def prepare(index, carry):
        basis = jnp.dot(
            lower_inverse[...],
            far[index].astype(jnp.float32),
            precision=lax.Precision.HIGHEST,
            preferred_element_type=jnp.float32,
        )
        scaled[index] = (basis * inverse[index]).astype(jnp.bfloat16)
        return carry

    lax.fori_loop(0, far.shape[0], prepare, 0, unroll=4)

    def one_tile(tile, carry):
        total = partial[tile]
        for slot in range(far_slots):
            total = total + jnp.dot(
                scaled[tile * far_slots + slot],
                kernel_half[tile, slot],
                preferred_element_type=jnp.float32,
            )
        raw[:, pl.ds(pl.multiple_of(tile * size, size), size)] = total / degree[tile]
        return carry

    lax.fori_loop(0, tiles, one_tile, 0, unroll=2)
    gram[...] = nt_dot(raw[...], raw[...], lax.Precision.HIGHEST)


def far_apply(lower_inverse, far, inverse, degree, kernel_half, partial):
    tiles, columns, size = partial.shape
    return pl.pallas_call(
        functools.partial(far_apply_body, tiles),
        out_shape=(
            jax.ShapeDtypeStruct((columns, tiles * size), jnp.float32),
            jax.ShapeDtypeStruct((columns, columns), jnp.float32),
        ),
        in_specs=[VMEM] * 6,
        out_specs=(VMEM, VMEM),
        scratch_shapes=[pltpu.VMEM(far.shape, jnp.bfloat16)],
        name="far_apply",
    )(lower_inverse, far, inverse, degree, kernel_half, partial)


def reduce_body(nz, ny, local, out, parts_w, parts_y, parts_z, stage, sw, rw, sy, ry, sz, rz, sa, ra):
    row = lax.axis_index("rows")
    y = lax.axis_index("grp")
    w = row % PLANE
    z = row // PLANE

    def peer_w(step):
        other = (w + step) % PLANE
        return other, (z * PLANE + other, y)

    def peer_y(step):
        other = (y + step) % ny
        return other, (row, other)

    def peer_z(step):
        other = (z + step) % nz
        return other, (other * PLANE + w, y)

    barrier = pltpu.get_barrier_semaphore()
    for count, peer in ((PLANE, peer_w), (ny, peer_y), (nz, peer_z)):

        def greet(step, carry):
            pl.semaphore_signal(barrier, inc=1, device_id=peer(step)[1], device_id_type=MESH)
            return carry

        lax.fori_loop(1, count, greet, 0)
    pl.semaphore_wait(barrier, PLANE + ny + nz - 3)

    def exchange(count, peer, me, source, target, send, recv):
        def copy(step, mine):
            other, device = peer(step)
            return pltpu.make_async_remote_copy(
                src_ref=source(other),
                dst_ref=target.at[me if mine else other],
                send_sem=send.at[other],
                recv_sem=recv.at[me if mine else other],
                device_id=device,
                device_id_type=MESH,
            )

        def start(step, carry):
            copy(step, True).start()
            return carry

        def finish(step, carry):
            copy(step, True).wait_send()
            copy(step, False).wait_recv()
            return carry

        lax.fori_loop(1, count, start, 0)
        lax.fori_loop(1, count, finish, 0)

    exchange(PLANE, peer_w, w, lambda other: local.at[other], parts_w, sw, rw)
    parts_w[w] = local[w]
    stage[0] = jnp.sum(parts_w[...], axis=0)
    exchange(ny, peer_y, y, lambda other: stage.at[0], parts_y, sy, ry)
    parts_y[y] = stage[0]
    stage[1] = jnp.sum(parts_y[...], axis=0)
    exchange(nz, peer_z, z, lambda other: stage.at[1], parts_z, sz, rz)
    parts_z[z] = stage[1]
    stage[2] = jnp.sum(parts_z[...], axis=0)
    exchange(PLANE, peer_w, w, lambda other: stage.at[2], out, sa, ra)
    out[w] = stage[2]


def total_gram(gram):
    columns = gram.shape[0]
    height = columns // PLANE
    ny = lax.axis_size("grp")
    nz = lax.axis_size("rows") // PLANE
    chunk = (height, columns)
    dma = pltpu.SemaphoreType.DMA
    out = pl.pallas_call(
        functools.partial(reduce_body, nz, ny),
        out_shape=jax.ShapeDtypeStruct((PLANE,) + chunk, jnp.float32),
        in_specs=[VMEM],
        out_specs=VMEM,
        scratch_shapes=[
            pltpu.VMEM((PLANE,) + chunk, jnp.float32),
            pltpu.VMEM((ny,) + chunk, jnp.float32),
            pltpu.VMEM((nz,) + chunk, jnp.float32),
            pltpu.VMEM((3,) + chunk, jnp.float32),
            dma((PLANE,)),
            dma((PLANE,)),
            dma((ny,)),
            dma((ny,)),
            dma((nz,)),
            dma((nz,)),
            dma((PLANE,)),
            dma((PLANE,)),
        ],
        compiler_params=pltpu.CompilerParams(collective_id=0, has_side_effects=True),
        name="gram_reduce",
    )(gram.reshape((PLANE,) + chunk))
    return out.reshape(columns, columns)


def lower_inverse_of(gram, total_rows):
    lower = jnp.linalg.cholesky(total_gram(gram) / total_rows)
    identity = jnp.eye(gram.shape[0], dtype=jnp.float32)
    return lax.linalg.triangular_solve(lower, identity, left_side=True, lower=True)


def exchange_tiles(tiles, requested, owner):
    sent = jnp.take(tiles, requested, axis=0, mode="clip")
    got = lax.all_to_all(sent, "rows", split_axis=0, concat_axis=0, tiled=True)
    return jnp.take(got, owner, axis=0, mode="clip")


def shards(features, length_scale, prior, partners, counts, projection):
    tiles, slots = partners.shape[1:]
    size = features.shape[1] // tiles
    columns = projection.shape[1]
    nrows = lax.axis_size("rows")
    device_index = lax.axis_index("rows")
    own_rows = features[0].reshape(tiles, size, features.shape[2])
    own_side = jnp.stack(
        [length_scale[0].reshape(tiles, size), prior[0].reshape(tiles, size)], axis=1
    )
    lists = partners[0]
    far_tiles = lists[:, NEAR:].reshape(-1)
    owner = far_tiles // tiles
    hits = owner[:, None] == jnp.arange(nrows, dtype=jnp.int32)[None, :]
    wanted = jnp.sum(jnp.where(hits, (far_tiles % tiles)[:, None], 0), axis=0)
    requested = lax.all_to_all(wanted, "rows", split_axis=0, concat_axis=0, tiled=True)
    table = (lists - device_index * tiles).reshape(-1)

    far_side = exchange_tiles(own_side, requested, owner).astype(jnp.float32)
    far_rows = exchange_tiles(own_rows, requested, owner)
    side = own_side.astype(jnp.float32)
    own_band, own_prior = side[:, 0:1, :], side[:, 1:2, :]
    far_band, far_prior = far_side[:, 0:1, :], far_side[:, 1:2, :]
    directions = projection.T
    near_half, near_density, norms = near_kernel(table, counts[0], own_rows, own_band, slots)
    far_half, own_inverse = far_kernel(
        counts[0], own_rows, own_band, far_rows, far_band, norms, near_density, slots
    )
    far_inverse = exchange_tiles(own_inverse.astype(jnp.bfloat16), requested, owner)
    far_inverse = far_inverse.astype(jnp.float32)
    near_part = near_walk(table, own_rows, own_prior, own_inverse, directions, near_half, slots)
    raw, raw_half, degree, gram = far_walk(
        far_rows, far_prior, far_inverse, directions, far_half, near_part
    )
    far_raw = exchange_tiles(raw_half, requested, owner)
    total_rows = nrows * lax.axis_size("grp") * tiles * size
    lower_inverse = lower_inverse_of(gram, total_rows)
    basis, near_second = near_apply(table, lower_inverse, raw, own_inverse, near_half, slots)
    second_raw, second_gram = far_apply(
        lower_inverse, far_raw, far_inverse, degree, far_half, near_second
    )
    embedding = jnp.dot(
        lower_inverse_of(second_gram, total_rows), second_raw, precision=lax.Precision.HIGHEST
    )
    return basis[None], embedding[None]


def solution(mesh):
    in_specs = (
        P("grp", "rows", None),
        P("grp", "rows"),
        P("grp", "rows"),
        P("grp", "rows", None),
        P("grp", "rows"),
        P(),
    )
    out_specs = (P("grp", None, "rows"), P("grp", None, "rows"))
    return jax.shard_map(shards, mesh=mesh, in_specs=in_specs, out_specs=out_specs, check_vma=False)
```

time: 533 us -> 495 us (0.929)
  blocking collectives: 130 us -> 0 us
  Pallas kernels: 105 us -> 180 us
  starting transfers between devices: 32.8 us -> 55.2 us
    all_to_all x2 -> x0, blocking collectives: 130 us -> none  [exchange_tiles(): got = lax.all_to_all(sent, 'rows', split_axis=0, concat_axis=0, tiled=True)]
    pallas_call x2, Pallas kernels: 56.3 us -> 138 us  [total_gram(): pl.pallas_call(functools.partial(reduce_body, nz, ny), out_shape=jax.Shap...]
    all_to_all x2 -> x4, starting transfers between devices: 12.4 us -> 34.8 us  [exchange_tiles(): got = lax.all_to_all(sent, 'rows', split_axis=0, concat_axis=0, tiled=True)]
    pallas_call x4 -> x6, Pallas kernels: 49.1 us -> 42.7 us  [the longest x1 10.8 us: near_kernel(): pl.pallas_call(functools.partial(near_kernel_body, tiles, slots), out_sha...]
    all_to_all x2 -> x4, waiting for transfers between devices: 193 us -> 189 us  [exchange_tiles(): got = lax.all_to_all(sent, 'rows', split_axis=0, concat_axis=0, tiled=True)]
  transfers between devices with their start and end apart: 3 -> 5, of which waited for: 3 -> 4; matrix products, arithmetic and copies ran while one was open for 1% -> 4% of each run, Pallas kernels for 0% -> 27%
where the time goes in v2:
time: 495 us; the launch traced here: 494 us
  waiting for transfers between devices  203 us (41%)
  Pallas kernels  180 us (36%)
  starting transfers between devices  55.2 us (11%)
  other arithmetic  31.3 us (6%)
  local copies, waits for them, and re-layouts  20.2 us (4%)
    all_to_all x4, waiting for transfers between devices, exchange_tiles(): got = lax.all_to_all(sent, 'rows', split_axis=0, concat_axis=0, tiled=True)  189 us
    pallas_call x2, Pallas kernels, total_gram(): pl.pallas_call(functools.partial(reduce_body, nz, ny), out_shape=jax.Shap...  138 us
    all_to_all x4, starting transfers between devices, exchange_tiles(): got = lax.all_to_all(sent, 'rows', split_axis=0, concat_axis=0, tiled=True)  34.8 us
    all_to_all x1, starting transfers between devices, shards(): lax.all_to_all(wanted, 'rows', split_axis=0, concat_axis=0, tiled=True)  20.4 us
    all_to_all x1, waiting for transfers between devices, shards(): lax.all_to_all(wanted, 'rows', split_axis=0, concat_axis=0, tiled=True)  14.1 us
    another operation x6, other arithmetic, lower_inverse_of(): lower = jnp.linalg.cholesky(total_gram(gram) / total_rows)  13 us
    another operation x4, other arithmetic, lower_inverse_of(): lax.linalg.triangular_solve(lower, identity, left_side=True, lower=True)  11.1 us
    pallas_call x1, Pallas kernels, near_kernel(): pl.pallas_call(functools.partial(near_kernel_body, tiles, slots), out_sha...  10.8 us
  transfers between devices with their start and end apart: 5, of which 4 were waited for; matrix products, arithmetic and copies ran while one was open for 4% of the time, Pallas kernels for 27%

profile of v2, /device:TPU:1, one launch (start us, length us, event | category | flops | bytes accessed | tf_op | source)
XLA Modules:
  0.0 494.2 jit_solution(113264381160930899)
XLA Ops:
  0.6 0.7 copy.32
  1.9 0.7 copy.21
  2.7 20.4 %all-to-all-start = ((s32[128,1,1]{2,1,0:T(1,128)}), s32[128,1,1]{2,1,0:T(1,128)S(1)}, u32[]{:S(2)}, u32[]{:S(2)}) async-start(s32[128,1,1]{2,1,0:T(1,128)} %copy.21), calls=%async_computation | async-start | bytes 131072 | tf_op jit(solution)/shard_map/all_to_all | solution.py:462
  23.1 0.7 pad_maximum_fusion
  23.8 14.1 %all-to-all-done = s32[128,1,1]{2,1,0:T(1,128)S(1)} async-done(((s32[128,1,1]{2,1,0:T(1,128)}), s32[128,1,1]{2,1,0:T(1,128)S(1)}, u32[]{:S(2)}, u32[]{:S(2)}) %all-to-all-start) | async-done | bytes 544 | tf_op jit(solution)/shard_map/all_to_all | solution.py:462
  37.9 2.3 reduce.5
  40.3 1.4 gather_fusion.2
  41.6 5.6 %all-to-all-start.2 = ((bf16[128,2,128]{2,1,0:T(2,128)(2,1)}), bf16[128,2,128]{2,1,0:T(2,128)(2,1)S(1)}, u32[]{:S(2)}, u32[]{:S(2)}) async-start(bf16[128,2,128]{2,1,0:T(2,128)(2,1)} %gather_fusion.2), calls=%async_computation.2 | async-start | bytes 131072 | tf_op jit(solution)/shard_map/all_to_all | solution.py:443
  47.3 3.1 gather_fusion
  50.4 11.9 %all-to-all-done.2 = bf16[128,2,128]{2,1,0:T(2,128)(2,1)S(1)} async-done(((bf16[128,2,128]{2,1,0:T(2,128)(2,1)}), bf16[128,2,128]{2,1,0:T(2,128)(2,1)S(1)}, u32[]{:S(2)}, u32[]{:S(2)}) %all-to-all-start.2) | async-done | bytes 65568 | tf_op jit(solution)/shard_map/all_to_all | solution.py:443
  62.3 6.7 %all-to-all-start.1 = ((bf16[128,128,128]{2,1,0:T(8,128)(2,1)}), bf16[128,128,128]{2,1,0:T(8,128)(2,1)}, u32[]{:S(2)}, u32[]{:S(2)}) async-start(bf16[128,128,128]{2,1,0:T(8,128)(2,1)} %gather_fusion), calls=%async_computation.1 | async-start | bytes 8388608 | tf_op jit(solution)/shard_map/all_to_all | solution.py:443
  69.2 0.6 sub.20.table
  69.9 0.6 fusion.12
  70.5 10.8 %near_kernel.1 = (bf16[12,13,128,128]{3,2,1,0:T(8,128)(2,1)}, f32[12,1,128]{2,1,0:T(1,128)}, f32[12,1,128]{2,1,0:T(1,128)}) custom-call(s32[192]{0:T(256)} %sub.20.table, s32[12]{0:T(128)} %bitcast.66, bf16[12,128,128]{2,1,0:T(8,128)(2,1)} %bitcast.51, f32[12,1,128]{2,1,0:T(1,128)} %get-tuple-element.37.band), custom_call_target="tpu_custom_call" | custom-call | flops 1022361600 | bytes 10223616 | tf_op jit(solution)/shard_map/near_kernel/pallas_call | solution.py:83
  81.3 0.6 gather_fusion.3
  81.9 0.6 fusion.11
  82.6 170.2 %all-to-all-done.1 = bf16[128,128,128]{2,1,0:T(8,128)(2,1)} async-done(((bf16[128,128,128]{2,1,0:T(8,128)(2,1)}), bf16[128,128,128]{2,1,0:T(8,128)(2,1)}, u32[]{:S(2)}, u32[]{:S(2)}) %all-to-all-start.1) | async-done | bytes 4194336 | tf_op jit(solution)/shard_map/all_to_all | solution.py:443
  252.7 4.0 gather_fusion.1
  256.7 4.8 far_kernel.1
  261.5 0.7 convert_element_type.20
  262.2 0.7 gather_fusion.4
  262.9 0.7 copy.22
  263.6 13.1 %all-to-all-start.3 = ((bf16[128,1,128]{2,1,0:T(2,128)(2,1)}), bf16[128,1,128]{2,1,0:T(2,128)(2,1)S(1)}, u32[]{:S(2)}, u32[]{:S(2)}) async-start(bf16[128,1,128]{2,1,0:T(2,128)(2,1)} %copy.22), calls=%async_computation.3 | async-start | bytes 131072 | tf_op jit(solution)/shard_map/all_to_all | solution.py:443
  276.7 8.0 %near_walk.1.partial = f32[12,80,128]{2,1,0:T(8,128)} custom-call(s32[192]{0:T(256)} %sub.20.table, bf16[12,128,128]{2,1,0:T(8,128)(2,1)} %bitcast.53, f32[12,1,128]{2,1,0:T(1,128)} %get-tuple-element.36.prior, f32[12,1,128]{2,1,0:T(1,128)} %get-tuple-element.19.inverse, bf16[64,128]{1,0:T(8,128)(2,1)} %bitcast.60, ...), custom_call_target="tpu_custom_call" | custom-call | flops 408944640 | bytes 10223616 | tf_op jit(solution)/shard_map/near_walk/pallas_call | solution.py:182
  284.7 6.8 %all-to-all-done.3 = bf16[128,1,128]{2,1,0:T(2,128)(2,1)S(1)} async-done(((bf16[128,1,128]{2,1,0:T(2,128)(2,1)}), bf16[128,1,128]{2,1,0:T(2,128)(2,1)S(1)}, u32[]{:S(2)}, u32[]{:S(2)}) %all-to-all-start.3) | async-done | bytes 32800 | tf_op jit(solution)/shard_map/all_to_all | solution.py:443
  292.1 0.6 reshape.185.inverse
  292.7 6.1 %far_walk.1 = (f32[64,1536]{1,0:T(8,128)}, bf16[12,64,128]{2,1,0:T(8,128)(2,1)}, f32[12,1,128]{2,1,0:T(1,128)}, f32[64,64]{1,0:T(8,128)}) custom-call(bf16[36,128,128]{2,1,0:T(8,128)(2,1)} %gather_fusion.1, f32[36,1,128]{2,1,0:T(1,128)} %get-tuple-element.33.prior, f32[36,1,128]{2,1,0:T(1,128)} %reshape.185.inverse, bf16[64,128]{1,0:T(8,128)(2,1)} %bitcast.61, ...), custom_call_target="tpu_custom_call" | custom-call | tf_op jit(solution)/shard_map/far_walk/pallas_call | solution.py:231
  298.8 3.1 gather_fusion.6
  301.9 9.3 %all-to-all-start.4 = ((bf16[128,64,128]{2,1,0:T(8,128)(2,1)}), bf16[128,64,128]{2,1,0:T(8,128)(2,1)S(1)}, u32[]{:S(2)}, u32[]{:S(2)}) async-start(bf16[128,64,128]{2,1,0:T(8,128)(2,1)} %gather_fusion.6), calls=%async_computation.4 | async-start | bytes 4194304 | tf_op jit(solution)/shard_map/all_to_all | solution.py:443
  311.2 109.6 %gram_reduce.2 = f32[8,8,64]{2,1,0:T(8,128)} custom-call(f32[8,8,64]{2,1,0:T(8,128)} %bitcast.62), custom_call_target="tpu_custom_call" | custom-call | tf_op jit(solution)/shard_map/gram_reduce/pallas_call | solution.py:410
  420.8 0.8 multiply_bitcast_fusion.1
  421.6 0.8 fusion.9
  422.4 5.8 %cholesky.44 = f32[64,64]{1,0:T(8,128)S(1)} custom-call(f32[64,64]{1,0:T(8,128)S(1)} %fusion.9), custom_call_target="Cholesky" | custom-call | tf_op jit(solution)/shard_map/jit(cholesky)/cholesky | solution.py:436
  428.3 0.6 compare_reduce_fusion.1
  428.9 0.7 fusion.4
  429.6 4.9 custom-call.6
  434.5 0.9 fusion.2.lower_inverse
  435.3 7.0 %near_apply.1 = (f32[64,1536]{1,0:T(8,128)}, f32[12,64,128]{2,1,0:T(8,128)}) custom-call(s32[192]{0:T(256)} %sub.20.table, f32[64,64]{1,0:T(8,128)} %fusion.2.lower_inverse, f32[64,1536]{1,0:T(8,128)} %get-tuple-element.23.raw, f32[12,1,128]{2,1,0:T(1,128)} %get-tuple-element.19.inverse, bf16[12,13,128,128]{3,2,1,0:T(8,128)(2,1)} %get-tuple-element.21.kernel_half), custom_call_target="tpu_custom_call" | custom-call | flops 327155712 | bytes 10223616 | tf_op jit(solution)/shard_map/near_apply/pallas_call | solution.py:278
  442.3 1.5 gather_fusion.7
  443.8 6.0 %far_apply.1 = (f32[64,1536]{1,0:T(8,128)}, f32[64,64]{1,0:T(8,128)}) custom-call(f32[64,64]{1,0:T(8,128)} %fusion.2.lower_inverse, bf16[36,64,128]{2,1,0:T(8,128)(2,1)} %gather_fusion.7, f32[36,1,128]{2,1,0:T(1,128)} %reshape.185.inverse, f32[12,1,128]{2,1,0:T(1,128)} %get-tuple-element.26.degree, bf16[12,3,128,128]{3,2,1,0:T(8,128)(2,1)} %get-tuple-element.20.kernel_half, ...), custom_call_target="tpu_custom_call" | custom-call | tf_op jit(solution)/shard_map/far_apply/pallas_call | solution.py:325
  449.8 28.2 %gram_reduce.3 = f32[8,8,64]{2,1,0:T(8,128)} custom-call(f32[8,8,64]{2,1,0:T(8,128)} %bitcast.63), custom_call_target="tpu_custom_call" | custom-call | tf_op jit(solution)/shard_map/gram_reduce/pallas_call | solution.py:410
  478.0 0.8 multiply_bitcast_fusion
  478.9 0.8 fusion.7
  479.7 5.8 %cholesky.55 = f32[64,64]{1,0:T(8,128)S(1)} custom-call(f32[64,64]{1,0:T(8,128)S(1)} %fusion.7), custom_call_target="Cholesky" | custom-call | tf_op jit(solution)/shard_map/jit(cholesky)/cholesky | solution.py:436
  485.5 0.6 compare_reduce_fusion
  486.2 0.7 fusion.5
  486.8 4.9 custom-call.7
  492.0 2.2 convolution_bitcast_fusion
  (26 shorter events, 1.8 us)
Async XLA Ops:
  0.6 46.7 %copy-start = (bf16[1,1536,128]{2,1,0:T(8,128)(2,1)S(1)}, bf16[1,1536,128]{2,1,0:T(8,128)(2,1)}, u32[]{:S(2)}) copy-start(bf16[1,1536,128]{2,1,0:T(8,128)(2,1)} %param.9) | copy-start | bytes 1179652
  2.7 35.2 %all-to-all-start = ((s32[128,1,1]{2,1,0:T(1,128)}), s32[128,1,1]{2,1,0:T(1,128)S(1)}, u32[]{:S(2)}, u32[]{:S(2)}) async-start(s32[128,1,1]{2,1,0:T(1,128)} %copy.21), calls=%async_computation | async-start | bytes 131072 | tf_op jit(solution)/shard_map/all_to_all | solution.py:462
  41.6 20.7 %all-to-all-start.2 = ((bf16[128,2,128]{2,1,0:T(2,128)(2,1)}), bf16[128,2,128]{2,1,0:T(2,128)(2,1)S(1)}, u32[]{:S(2)}, u32[]{:S(2)}) async-start(bf16[128,2,128]{2,1,0:T(2,128)(2,1)} %gather_fusion.2), calls=%async_computation.2 | async-start | bytes 131072 | tf_op jit(solution)/shard_map/all_to_all | solution.py:443
  50.4 18.7 %copy-start.1 = (s32[1,12,16]{2,0,1:T(1,128)S(1)}, s32[1,12,16]{2,0,1:T(1,128)}, u32[]{:S(2)}) copy-start(s32[1,12,16]{2,0,1:T(1,128)} %param.12) | copy-start | bytes 2308
  62.3 190.4 %all-to-all-start.1 = ((bf16[128,128,128]{2,1,0:T(8,128)(2,1)}), bf16[128,128,128]{2,1,0:T(8,128)(2,1)}, u32[]{:S(2)}, u32[]{:S(2)}) async-start(bf16[128,128,128]{2,1,0:T(8,128)(2,1)} %gather_fusion), calls=%async_computation.1 | async-start | bytes 8388608 | tf_op jit(solution)/shard_map/all_to_all | solution.py:443
  263.6 27.9 %all-to-all-start.3 = ((bf16[128,1,128]{2,1,0:T(2,128)(2,1)}), bf16[128,1,128]{2,1,0:T(2,128)(2,1)S(1)}, u32[]{:S(2)}, u32[]{:S(2)}) async-start(bf16[128,1,128]{2,1,0:T(2,128)(2,1)} %copy.22), calls=%async_computation.3 | async-start | bytes 131072 | tf_op jit(solution)/shard_map/all_to_all | solution.py:443
  301.9 140.4 %all-to-all-start.4 = ((bf16[128,64,128]{2,1,0:T(8,128)(2,1)}), bf16[128,64,128]{2,1,0:T(8,128)(2,1)S(1)}, u32[]{:S(2)}, u32[]{:S(2)}) async-start(bf16[128,64,128]{2,1,0:T(8,128)(2,1)} %gather_fusion.6), calls=%async_computation.4 | async-start | bytes 4194304 | tf_op jit(solution)/shard_map/all_to_all | solution.py:443

commit v3 on v2

--- a/solution.py
+++ b/solution.py
@@ -398,6 +398,62 @@
     stage[2] = jnp.sum(parts_z[...], axis=0)
     exchange(PLANE, peer_w, w, lambda other: stage.at[2], out, sa, ra)
     out[w] = stage[2]
+
+
+def swap_body(count, sent, got, send, recv):
+    me = lax.axis_index("rows")
+    y = lax.axis_index("grp")
+
+    def other_of(step):
+        return (me + step) % count
+
+    barrier = pltpu.get_barrier_semaphore()
+
+    def greet(step, carry):
+        pl.semaphore_signal(barrier, inc=1, device_id=(other_of(step), y), device_id_type=MESH)
+        return carry
+
+    lax.fori_loop(1, count, greet, 0)
+    pl.semaphore_wait(barrier, count - 1)
+
+    def copy(step, mine):
+        other = other_of(step)
+        slot = me if mine else other
+        return pltpu.make_async_remote_copy(
+            src_ref=sent.at[other],
+            dst_ref=got.at[slot],
+            send_sem=send.at[other],
+            recv_sem=recv.at[slot],
+            device_id=(other, y),
+            device_id_type=MESH,
+        )
+
+    def start(step, carry):
+        copy(step, True).start()
+        return carry
+
+    def finish(step, carry):
+        copy(step, True).wait_send()
+        copy(step, False).wait_recv()
+        return carry
+
+    lax.fori_loop(1, count, start, 0)
+    got[me] = sent[me]
+    lax.fori_loop(1, count, finish, 0)
+
+
+def swap(sent, collective_id):
+    count = sent.shape[0]
+    dma = pltpu.SemaphoreType.DMA
+    return pl.pallas_call(
+        functools.partial(swap_body, count),
+        out_shape=jax.ShapeDtypeStruct(sent.shape, sent.dtype),
+        in_specs=[VMEM],
+        out_specs=VMEM,
+        scratch_shapes=[dma((count,)), dma((count,))],
+        compiler_params=pltpu.CompilerParams(collective_id=collective_id, has_side_effects=True),
+        name="swap_%d" % collective_id,
+    )(sent)
 
 
 def total_gram(gram):
@@ -433,7 +489,7 @@
 
 
 def lower_inverse_of(gram, total_rows):
-    lower = jnp.linalg.cholesky(total_gram(gram) / total_rows)
+    lower = jnp.linalg.cholesky(gram / total_rows)
     identity = jnp.eye(gram.shape[0], dtype=jnp.float32)
     return lax.linalg.triangular_solve(lower, identity, left_side=True, lower=True)
 
@@ -459,16 +515,20 @@
     owner = far_tiles // tiles
     hits = owner[:, None] == jnp.arange(nrows, dtype=jnp.int32)[None, :]
     wanted = jnp.sum(jnp.where(hits, (far_tiles % tiles)[:, None], 0), axis=0)
-    requested = lax.all_to_all(wanted, "rows", split_axis=0, concat_axis=0, tiled=True)
+    wide = jnp.broadcast_to(wanted[:, None, None], (nrows, 1, 128))
+    requested = swap(wide, 1)[:, 0, 0]
     table = (lists - device_index * tiles).reshape(-1)
 
-    far_side = exchange_tiles(own_side, requested, owner).astype(jnp.float32)
     far_rows = exchange_tiles(own_rows, requested, owner)
     side = own_side.astype(jnp.float32)
     own_band, own_prior = side[:, 0:1, :], side[:, 1:2, :]
-    far_band, far_prior = far_side[:, 0:1, :], far_side[:, 1:2, :]
     directions = projection.T
     near_half, near_density, norms = near_kernel(table, counts[0], own_rows, own_band, slots)
+    near_density, far_side = lax.optimization_barrier(
+        (near_density, jnp.take(own_side, requested, axis=0, mode="clip"))
+    )
+    far_side = jnp.take(swap(far_side, 2), owner, axis=0, mode="clip").astype(jnp.float32)
+    far_band, far_prior = far_side[:, 0:1, :], far_side[:, 1:2, :]
     far_half, own_inverse = far_kernel(
         counts[0], own_rows, own_band, far_rows, far_band, norms, near_density, slots
     )
@@ -478,7 +538,11 @@
     raw, raw_half, degree, gram = far_walk(
         far_rows, far_prior, far_inverse, directions, far_half, near_part
     )
-    far_raw = exchange_tiles(raw_half, requested, owner)
+    middle = columns // 2
+    low_raw = exchange_tiles(raw_half[:, :middle], requested, owner)
+    gram, late_half = lax.optimization_barrier((total_gram(gram), raw_half[:, middle:]))
+    high_raw = exchange_tiles(late_half, requested, owner)
+    far_raw = jnp.concatenate([low_raw, high_raw], axis=1)
     total_rows = nrows * lax.axis_size("grp") * tiles * size
     lower_inverse = lower_inverse_of(gram, total_rows)
     basis, near_second = near_apply(table, lower_inverse, raw, own_inverse, near_half, slots)
@@ -486,7 +550,9 @@
         lower_inverse, far_raw, far_inverse, degree, far_half, near_second
     )
     embedding = jnp.dot(
-        lower_inverse_of(second_gram, total_rows), second_raw, precision=lax.Precision.HIGHEST
+        lower_inverse_of(total_gram(second_gram), total_rows),
+        second_raw,
+        precision=lax.Precision.HIGHEST,
     )
     return basis[None], embedding[None]
 

time: 495 us -> 485 us (0.980)
  Pallas kernels: 180 us -> 353 us
  waiting for transfers between devices: 203 us -> 38.4 us
  starting transfers between devices: 55.2 us -> 34.2 us
  local copies, waits for them, and re-layouts: 20.2 us -> 26.4 us
    pallas_call x0 -> x2, Pallas kernels: none -> 215 us  [swap(): pl.pallas_call(functools.partial(swap_body, count), out_shape=jax.ShapeDt...]
    all_to_all x4, waiting for transfers between devices: 189 us -> 38.4 us  [exchange_tiles(): got = lax.all_to_all(sent, 'rows', split_axis=0, concat_axis=0, tiled=True)]
    pallas_call x2, Pallas kernels: 138 us -> 95.5 us  [total_gram(): pl.pallas_call(functools.partial(reduce_body, nz, ny), out_shape=jax.Shap...]
    all_to_all x1 -> x0, starting transfers between devices: 20.4 us -> none  [shards(): lax.all_to_all(wanted, 'rows', split_axis=0, concat_axis=0, tiled=True)]
    all_to_all x1 -> x0, waiting for transfers between devices: 14.1 us -> none  [shards(): lax.all_to_all(wanted, 'rows', split_axis=0, concat_axis=0, tiled=True)]
  transfers between devices with their start and end apart: 5 -> 4, of which waited for: 4 -> 2; matrix products, arithmetic and copies ran while one was open for 4% -> 4% of each run, Pallas kernels for 27% -> 57%
where the time goes in v3:
time: 485 us; the launch traced here: 484 us
  Pallas kernels  353 us (73%)
  waiting for transfers between devices  38.4 us (8%)
  starting transfers between devices  34.2 us (7%)
  other arithmetic  27.6 us (6%)
  local copies, waits for them, and re-layouts  26.4 us (5%)
    pallas_call x2, Pallas kernels, swap(): pl.pallas_call(functools.partial(swap_body, count), out_shape=jax.ShapeDt...  215 us
    pallas_call x2, Pallas kernels, total_gram(): pl.pallas_call(functools.partial(reduce_body, nz, ny), out_shape=jax.Shap...  95.5 us
    all_to_all x4, waiting for transfers between devices, exchange_tiles(): got = lax.all_to_all(sent, 'rows', split_axis=0, concat_axis=0, tiled=True)  38.4 us
    all_to_all x4, starting transfers between devices, exchange_tiles(): got = lax.all_to_all(sent, 'rows', split_axis=0, concat_axis=0, tiled=True)  34.2 us
    another operation x6, other arithmetic, lower_inverse_of(): lower = jnp.linalg.cholesky(gram / total_rows)  13 us
    another operation x4, other arithmetic, lower_inverse_of(): lax.linalg.triangular_solve(lower, identity, left_side=True, lower=True)  11.1 us
    pallas_call x1, Pallas kernels, near_kernel(): pl.pallas_call(functools.partial(near_kernel_body, tiles, slots), out_sha...  10.8 us
  transfers between devices with their start and end apart: 4, of which 2 were waited for; matrix products, arithmetic and copies ran while one was open for 4% of the time, Pallas kernels for 57%

profile of v3, /device:TPU:1, one launch (start us, length us, event | category | flops | bytes accessed | tf_op | source)
XLA Modules:
  0.0 483.7 jit_solution(17525475298728679821)
XLA Ops:
  0.6 0.7 copy.34
  1.9 0.8 broadcast_in_dim.50.sent
  2.7 30.5 %swap_1.1 = s32[128,1,128]{2,1,0:T(1,128)} custom-call(s32[128,1,128]{2,1,0:T(1,128)} %broadcast_in_dim.50.sent), custom_call_target="tpu_custom_call" | custom-call | tf_op jit(solution)/shard_map/swap_1/pallas_call | solution.py:448
  33.3 3.3 slice_reduce_fusion
  36.6 4.1 gather_fusion
  40.7 13.0 %all-to-all-start = ((bf16[128,128,128]{2,1,0:T(8,128)(2,1)}), bf16[128,128,128]{2,1,0:T(8,128)(2,1)}, u32[]{:S(2)}, u32[]{:S(2)}) async-start(bf16[128,128,128]{2,1,0:T(8,128)(2,1)} %gather_fusion), calls=%async_computation | async-start | bytes 8388608 | tf_op jit(solution)/shard_map/all_to_all | solution.py:499
  53.8 0.6 sub.20.table
  54.6 1.4 gather_fusion.2
  56.0 0.6 fusion.13
  56.6 10.8 %near_kernel.1 = (bf16[12,13,128,128]{3,2,1,0:T(8,128)(2,1)}, f32[12,1,128]{2,1,0:T(1,128)}, f32[12,1,128]{2,1,0:T(1,128)}) custom-call(s32[192]{0:T(256)} %sub.20.table, s32[12]{0:T(128)} %bitcast.63, bf16[12,128,128]{2,1,0:T(8,128)(2,1)} %bitcast.48, f32[12,1,128]{2,1,0:T(1,128)} %get-tuple-element.47.band), custom_call_target="tpu_custom_call" | custom-call | flops 1022361600 | bytes 10223616 | tf_op jit(solution)/shard_map/near_kernel/pallas_call | solution.py:83
  67.4 184.2 %swap_2.1 = bf16[128,2,128]{2,1,0:T(2,128)(2,1)} custom-call(bf16[128,2,128]{2,1,0:T(2,128)(2,1)} %gather_fusion.2), custom_call_target="tpu_custom_call" | custom-call | tf_op jit(solution)/shard_map/swap_2/pallas_call | solution.py:448
  251.6 1.4 gather_fusion.3
  253.1 0.6 fusion.12
  253.7 4.0 gather_fusion.1
  257.7 4.8 far_kernel.1
  262.5 0.7 convert_element_type.20
  263.2 0.7 gather_fusion.4
  263.9 0.7 copy.23
  264.6 6.3 %all-to-all-start.1 = ((bf16[128,1,128]{2,1,0:T(2,128)(2,1)}), bf16[128,1,128]{2,1,0:T(2,128)(2,1)S(1)}, u32[]{:S(2)}, u32[]{:S(2)}) async-start(bf16[128,1,128]{2,1,0:T(2,128)(2,1)} %copy.23), calls=%async_computation.1 | async-start | bytes 131072 | tf_op jit(solution)/shard_map/all_to_all | solution.py:499
  270.8 8.0 %near_walk.1.partial = f32[12,80,128]{2,1,0:T(8,128)} custom-call(s32[192]{0:T(256)} %sub.20.table, bf16[12,128,128]{2,1,0:T(8,128)(2,1)} %bitcast.50, f32[12,1,128]{2,1,0:T(1,128)} %get-tuple-element.46.prior, f32[12,1,128]{2,1,0:T(1,128)} %get-tuple-element.25.inverse, bf16[64,128]{1,0:T(8,128)(2,1)} %bitcast.57, ...), custom_call_target="tpu_custom_call" | custom-call | flops 408944640 | bytes 10223616 | tf_op jit(solution)/shard_map/near_walk/pallas_call | solution.py:182
  278.8 6.8 %all-to-all-done.1 = bf16[128,1,128]{2,1,0:T(2,128)(2,1)S(1)} async-done(((bf16[128,1,128]{2,1,0:T(2,128)(2,1)}), bf16[128,1,128]{2,1,0:T(2,128)(2,1)S(1)}, u32[]{:S(2)}, u32[]{:S(2)}) %all-to-all-start.1) | async-done | bytes 32800 | tf_op jit(solution)/shard_map/all_to_all | solution.py:499
  286.3 0.6 reshape.203.inverse
  286.9 6.1 %far_walk.1 = (f32[64,1536]{1,0:T(8,128)}, bf16[12,64,128]{2,1,0:T(8,128)(2,1)}, f32[12,1,128]{2,1,0:T(1,128)}, f32[64,64]{1,0:T(8,128)}) custom-call(bf16[36,128,128]{2,1,0:T(8,128)(2,1)} %gather_fusion.1, f32[36,1,128]{2,1,0:T(1,128)} %get-tuple-element.43.prior, f32[36,1,128]{2,1,0:T(1,128)} %reshape.203.inverse, bf16[64,128]{1,0:T(8,128)(2,1)} %bitcast.58, ...), custom_call_target="tpu_custom_call" | custom-call | tf_op jit(solution)/shard_map/far_walk/pallas_call | solution.py:231
  293.0 1.0 fusion.11
  293.9 1.7 gather_fusion.6
  295.6 9.3 %all-to-all-start.2 = ((bf16[128,32,128]{2,1,0:T(8,128)(2,1)}), bf16[128,32,128]{2,1,0:T(8,128)(2,1)S(1)}, u32[]{:S(2)}, u32[]{:S(2)}) async-start(bf16[128,32,128]{2,1,0:T(8,128)(2,1)} %gather_fusion.6), calls=%async_computation.2 | async-start | bytes 2097152 | tf_op jit(solution)/shard_map/all_to_all | solution.py:499
  304.9 64.5 %gram_reduce.2 = f32[8,8,64]{2,1,0:T(8,128)} custom-call(f32[8,8,64]{2,1,0:T(8,128)} %bitcast.59), custom_call_target="tpu_custom_call" | custom-call | tf_op jit(solution)/shard_map/gram_reduce/pallas_call | solution.py:466
  369.4 1.7 gather_fusion.8
  371.1 5.7 %all-to-all-start.3 = ((bf16[128,32,128]{2,1,0:T(8,128)(2,1)}), bf16[128,32,128]{2,1,0:T(8,128)(2,1)S(1)}, u32[]{:S(2)}, u32[]{:S(2)}) async-start(bf16[128,32,128]{2,1,0:T(8,128)(2,1)} %gather_fusion.8), calls=%async_computation.3 | async-start | bytes 2097152 | tf_op jit(solution)/shard_map/all_to_all | solution.py:499
  377.0 5.8 %cholesky.44 = f32[64,64]{1,0:T(8,128)S(1)} custom-call(f32[64,64]{1,0:T(8,128)S(1)} %fusion.9), custom_call_target="Cholesky" | custom-call | tf_op jit(solution)/shard_map/jit(cholesky)/cholesky | solution.py:492
  382.9 0.6 compare_reduce_fusion.1
  383.6 0.7 fusion.4
  384.2 4.9 %custom-call.6 = f32[1,64,64]{1,2,0:T(8,128)S(1)} custom-call(f32[1,64,64]{2,1,0:T(8,128)S(1)} %fusion.4), custom_call_target="InvertDiagBlocksLowerTriangular" | custom-call | tf_op jit(solution)/shard_map/triangular_solve/custom-call.0 | solution.py:494
  389.1 0.9 fusion.2.lower_inverse
  390.0 6.9 %near_apply.1 = (f32[64,1536]{1,0:T(8,128)}, f32[12,64,128]{2,1,0:T(8,128)}) custom-call(s32[192]{0:T(256)} %sub.20.table, f32[64,64]{1,0:T(8,128)} %fusion.2.lower_inverse, f32[64,1536]{1,0:T(8,128)} %get-tuple-element.31.raw, f32[12,1,128]{2,1,0:T(1,128)} %get-tuple-element.25.inverse, bf16[12,13,128,128]{3,2,1,0:T(8,128)(2,1)} %get-tuple-element.27.kernel_half), custom_call_target="tpu_custom_call" | custom-call | flops 327155712 | bytes 10223616 | tf_op jit(solution)/shard_map/near_apply/pallas_call | solution.py:278
  396.9 0.6 gather_fusion.7
  397.5 31.5 %all-to-all-done.3 = bf16[128,32,128]{2,1,0:T(8,128)(2,1)S(1)} async-done(((bf16[128,32,128]{2,1,0:T(8,128)(2,1)}), bf16[128,32,128]{2,1,0:T(8,128)(2,1)S(1)}, u32[]{:S(2)}, u32[]{:S(2)}) %all-to-all-start.3) | async-done | bytes 1048608 | tf_op jit(solution)/shard_map/all_to_all | solution.py:499
  429.1 0.6 gather_fusion.9
  429.7 0.9 pad_maximum_fusion.far
  430.6 6.0 %far_apply.1 = (f32[64,1536]{1,0:T(8,128)}, f32[64,64]{1,0:T(8,128)}) custom-call(f32[64,64]{1,0:T(8,128)} %fusion.2.lower_inverse, bf16[36,64,128]{2,1,0:T(8,128)(2,1)} %pad_maximum_fusion.far, f32[36,1,128]{2,1,0:T(1,128)} %reshape.203.inverse, f32[12,1,128]{2,1,0:T(1,128)} %get-tuple-element.34.degree, ...), custom_call_target="tpu_custom_call" | custom-call | tf_op jit(solution)/shard_map/far_apply/pallas_call | solution.py:325
  436.6 31.0 %gram_reduce.3 = f32[8,8,64]{2,1,0:T(8,128)} custom-call(f32[8,8,64]{2,1,0:T(8,128)} %bitcast.60), custom_call_target="tpu_custom_call" | custom-call | tf_op jit(solution)/shard_map/gram_reduce/pallas_call | solution.py:466
  467.6 0.8 multiply_bitcast_fusion
  468.4 0.8 fusion.7
  469.2 5.8 %cholesky.55 = f32[64,64]{1,0:T(8,128)S(1)} custom-call(f32[64,64]{1,0:T(8,128)S(1)} %fusion.7), custom_call_target="Cholesky" | custom-call | tf_op jit(solution)/shard_map/jit(cholesky)/cholesky | solution.py:492
  475.1 0.6 compare_reduce_fusion
  475.7 0.7 fusion.5
  476.4 4.9 %custom-call.7 = f32[1,64,64]{1,2,0:T(8,128)S(1)} custom-call(f32[1,64,64]{2,1,0:T(8,128)S(1)} %fusion.5), custom_call_target="InvertDiagBlocksLowerTriangular" | custom-call | tf_op jit(solution)/shard_map/triangular_solve/custom-call.0 | solution.py:494
  481.5 2.2 convolution_bitcast_fusion
  (35 shorter events, 1.9 us)
Async XLA Ops:
  40.7 13.1 %copy-start.1 = (s32[1,12,16]{2,0,1:T(1,128)S(1)}, s32[1,12,16]{2,0,1:T(1,128)}, u32[]{:S(2)}) copy-start(s32[1,12,16]{2,0,1:T(1,128)} %param.12) | copy-start | bytes 2308
  40.7 13.8 %copy-start.2 = (bf16[1,1536]{1,0:T(2,128)(2,1)S(1)}, bf16[1,1536]{1,0:T(2,128)(2,1)}, u32[]{:S(2)}) copy-start(bf16[1,1536]{1,0:T(2,128)(2,1)} %param.11) | copy-start | bytes 9220
  40.7 13.9 %copy-start.3 = (bf16[1,1536]{1,0:T(2,128)(2,1)S(1)}, bf16[1,1536]{1,0:T(2,128)(2,1)}, u32[]{:S(2)}) copy-start(bf16[1,1536]{1,0:T(2,128)(2,1)} %param.10) | copy-start | bytes 9220
  40.7 213.0 %all-to-all-start = ((bf16[128,128,128]{2,1,0:T(8,128)(2,1)}), bf16[128,128,128]{2,1,0:T(8,128)(2,1)}, u32[]{:S(2)}, u32[]{:S(2)}) async-start(bf16[128,128,128]{2,1,0:T(8,128)(2,1)} %gather_fusion), calls=%async_computation | async-start | bytes 8388608 | tf_op jit(solution)/shard_map/all_to_all | solution.py:499
  264.6 21.1 %all-to-all-start.1 = ((bf16[128,1,128]{2,1,0:T(2,128)(2,1)}), bf16[128,1,128]{2,1,0:T(2,128)(2,1)S(1)}, u32[]{:S(2)}, u32[]{:S(2)}) async-start(bf16[128,1,128]{2,1,0:T(2,128)(2,1)} %copy.23), calls=%async_computation.1 | async-start | bytes 131072 | tf_op jit(solution)/shard_map/all_to_all | solution.py:499
  295.6 75.5 %all-to-all-start.2 = ((bf16[128,32,128]{2,1,0:T(8,128)(2,1)}), bf16[128,32,128]{2,1,0:T(8,128)(2,1)S(1)}, u32[]{:S(2)}, u32[]{:S(2)}) async-start(bf16[128,32,128]{2,1,0:T(8,128)(2,1)} %gather_fusion.6), calls=%async_computation.2 | async-start | bytes 2097152 | tf_op jit(solution)/shard_map/all_to_all | solution.py:499
  371.1 5.7 %copy-start = (f32[8,8,64]{2,1,0:T(8,128)S(1)}, f32[8,8,64]{2,1,0:T(8,128)}, u32[]{:S(2)}) copy-start(f32[8,8,64]{2,1,0:T(8,128)} %gram_reduce.2) | copy-start | bytes 49156
  371.1 58.0 %all-to-all-start.3 = ((bf16[128,32,128]{2,1,0:T(8,128)(2,1)}), bf16[128,32,128]{2,1,0:T(8,128)(2,1)S(1)}, u32[]{:S(2)}, u32[]{:S(2)}) async-start(bf16[128,32,128]{2,1,0:T(8,128)(2,1)} %gather_fusion.8), calls=%async_computation.3 | async-start | bytes 2097152 | tf_op jit(solution)/shard_map/all_to_all | solution.py:499

commit v4 on v2

--- a/solution.py
+++ b/solution.py
@@ -95,8 +95,9 @@
     )(table, counts, pool, band)
 
 
-def far_kernel_body(tiles, slots, counts, pool, band, far, far_band, norm_a, near, kernel_half, inverse):
+def far_kernel_body(tiles, slots, counts, pool, band, far, norm_a, near, kernel_half, inverse):
     far_slots = slots - NEAR
+    size = pool.shape[1]
 
     def one_tile(tile, carry):
         doubled = pool[tile] * jnp.bfloat16(2)
@@ -104,11 +105,11 @@
         total = jnp.zeros((8, pool.shape[1]), jnp.float32)
         for slot in range(far_slots):
             index = tile * far_slots + slot
-            rows = far[index]
+            rows = far[index, 0:size, :]
             value = kernel_value(
                 rows,
                 load_norm(rows),
-                column_band(far_band[index]),
+                column_band(far[index, size : size + 1, :].astype(jnp.float32)),
                 doubled,
                 norm_a[tile],
                 band[tile],
@@ -122,7 +123,7 @@
     lax.fori_loop(0, tiles, one_tile, 0, unroll=2)
 
 
-def far_kernel(counts, pool, band, far, far_band, norm_a, near, slots):
+def far_kernel(counts, pool, band, far, norm_a, near, slots):
     tiles, size, _ = pool.shape
     return pl.pallas_call(
         functools.partial(far_kernel_body, tiles, slots),
@@ -130,10 +131,10 @@
             jax.ShapeDtypeStruct((tiles, slots - NEAR, size, size), jnp.bfloat16),
             jax.ShapeDtypeStruct((tiles, 1, size), jnp.float32),
         ),
-        in_specs=[SMEM] + [VMEM] * 6,
+        in_specs=[SMEM] + [VMEM] * 5,
         out_specs=(VMEM, VMEM),
         name="far_kernel",
-    )(counts, pool, band, far, far_band, norm_a, near)
+    )(counts, pool, band, far, norm_a, near)
 
 
 def cost(flops, scale):
@@ -191,15 +192,20 @@
 
 
 def far_walk_body(
-    tiles, far, prior, inverse, projection, kernel_half, partial, raw, half, degree, gram, scaled
+    tiles, far, inverse, projection, kernel_half, partial, raw, half, degree, gram, scaled
 ):
-    size = far.shape[1]
+    size = far.shape[2]
     columns = projection.shape[0]
     far_slots = kernel_half.shape[1]
     gram[...] = jnp.zeros_like(gram)
 
     def prepare(index, carry):
-        main, extra = scale_start(projection[...], far[index], prior[index], inverse[index])
+        main, extra = scale_start(
+            projection[...],
+            far[index, 0:size, :],
+            far[index, size + 1 : size + 2, :].astype(jnp.float32),
+            inverse[index],
+        )
         scaled[index, 0:columns, :] = main
         scaled[index, columns : columns + 16, :] = extra
         return carry
@@ -225,7 +231,7 @@
     gram[...] = nt_dot(raw[...], raw[...], lax.Precision.HIGHEST)
 
 
-def far_walk(far, prior, inverse, projection, kernel_half, partial):
+def far_walk(far, inverse, projection, kernel_half, partial):
     tiles, _, size, _ = kernel_half.shape
     columns = projection.shape[0]
     return pl.pallas_call(
@@ -236,19 +242,54 @@
             jax.ShapeDtypeStruct((tiles, 1, size), jnp.float32),
             jax.ShapeDtypeStruct((columns, columns), jnp.float32),
         ),
-        in_specs=[VMEM] * 6,
+        in_specs=[VMEM] * 5,
         out_specs=(VMEM,) * 4,
         scratch_shapes=[pltpu.VMEM((far.shape[0], columns + 16, size), jnp.bfloat16)],
         name="far_walk",
-    )(far, prior, inverse, projection, kernel_half, partial)
+    )(far, inverse, projection, kernel_half, partial)
+
+
+def lower_inverse_of(gram, total_rows):
+    count = gram.shape[0]
+    row = lax.broadcasted_iota(jnp.int32, (count, 2 * count), 0)
+    lane = lax.broadcasted_iota(jnp.int32, (count, 2 * count), 1)
+    identity = jnp.where(row == lane, 1.0, 0.0)[:, 0:count]
+    work = jnp.concatenate([identity, gram * (1.0 / total_rows)], axis=1)
+    for step in range(count - 1):
+        at = count + step
+        factor = work[:, at : at + 1] / work[step : step + 1, at : at + 1]
+        below = jnp.where(row[:, 0:1] > step, factor, 0.0)
+        work = work - below * work[step : step + 1, :]
+    pivots = jnp.sum(jnp.where(lane == row + count, work, 0.0), axis=1, keepdims=True)
+    return work[:, 0:count] / jnp.sqrt(pivots)
+
+
+def finish_body(total_rows, gram, raw, basis):
+    basis[...] = jnp.dot(
+        lower_inverse_of(gram[...], total_rows),
+        raw[...],
+        precision=lax.Precision.HIGHEST,
+        preferred_element_type=jnp.float32,
+    )
+
+
+def finish(gram, raw, total_rows):
+    return pl.pallas_call(
+        functools.partial(finish_body, total_rows),
+        out_shape=jax.ShapeDtypeStruct(raw.shape, jnp.float32),
+        in_specs=[VMEM, VMEM],
+        out_specs=VMEM,
+        name="finish",
+    )(gram, raw)
 
 
 def near_apply_body(
-    tiles, slots, table, lower_inverse, raw, inverse, kernel_half, basis, partial, scaled
+    tiles, slots, total_rows, table, gram, raw, inverse, kernel_half, basis, partial, lower, scaled
 ):
     size = inverse.shape[2]
+    lower[...] = lower_inverse_of(gram[...], total_rows)
     value = jnp.dot(
-        lower_inverse[...],
+        lower[...],
         raw[...],
         precision=lax.Precision.HIGHEST,
         preferred_element_type=jnp.float32,
@@ -272,21 +313,22 @@
     lax.fori_loop(0, tiles, one_tile, 0)
 
 
-def near_apply(table, lower_inverse, raw, inverse, kernel_half, slots):
+def near_apply(table, gram, raw, inverse, kernel_half, slots, total_rows):
     tiles, _, size, _ = kernel_half.shape
     columns = raw.shape[0]
     return pl.pallas_call(
-        functools.partial(near_apply_body, tiles, slots),
+        functools.partial(near_apply_body, tiles, slots, total_rows),
         out_shape=(
             jax.ShapeDtypeStruct(raw.shape, jnp.float32),
             jax.ShapeDtypeStruct((tiles, columns, size), jnp.float32),
+            jax.ShapeDtypeStruct(gram.shape, jnp.float32),
         ),
         in_specs=[SMEM] + [VMEM] * 4,
-        out_specs=(VMEM, VMEM),
+        out_specs=(VMEM, VMEM, VMEM),
         scratch_shapes=[pltpu.VMEM((tiles, columns, size), jnp.bfloat16)],
         cost_estimate=cost(tiles * NEAR * size * size, 128),
         name="near_apply",
-    )(table, lower_inverse, raw, inverse, kernel_half)
+    )(table, gram, raw, inverse, kernel_half)
 
 
 def far_apply_body(tiles, lower_inverse, far, inverse, degree, kernel_half, partial, raw, gram, scaled):
@@ -335,6 +377,44 @@
     )(lower_inverse, far, inverse, degree, kernel_half, partial)
 
 
+def exchange(count, peer, me, source, target, send, recv):
+    def copy(step, mine):
+        other, device = peer(step)
+        slot = me if mine else other
+        return pltpu.make_async_remote_copy(
+            src_ref=source(other),
+            dst_ref=target.at[slot],
+            send_sem=send.at[other],
+            recv_sem=recv.at[slot],
+            device_id=device,
+            device_id_type=MESH,
+        )
+
+    def start(step, carry):
+        copy(step, True).start()
+        return carry
+
+    def finish(step, carry):
+        copy(step, True).wait_send()
+        copy(step, False).wait_recv()
+        return carry
+
+    lax.fori_loop(1, count, start, 0)
+    lax.fori_loop(1, count, finish, 0)
+
+
+def greet_all(groups):
+    barrier = pltpu.get_barrier_semaphore()
+    for count, peer in groups:
+
+        def greet(step, carry):
+            pl.semaphore_signal(barrier, inc=1, device_id=peer(step)[1], device_id_type=MESH)
+            return carry
+
+        lax.fori_loop(1, count, greet, 0)
+    pl.semaphore_wait(barrier, sum(count - 1 for count, _ in groups))
+
+
 def reduce_body(nz, ny, local, out, parts_w, parts_y, parts_z, stage, sw, rw, sy, ry, sz, rz, sa, ra):
     row = lax.axis_index("rows")
     y = lax.axis_index("grp")
@@ -353,40 +433,7 @@
         other = (z + step) % nz
         return other, (other * PLANE + w, y)
 
-    barrier = pltpu.get_barrier_semaphore()
-    for count, peer in ((PLANE, peer_w), (ny, peer_y), (nz, peer_z)):
-
-        def greet(step, carry):
-            pl.semaphore_signal(barrier, inc=1, device_id=peer(step)[1], device_id_type=MESH)
-            return carry
-
-        lax.fori_loop(1, count, greet, 0)
-    pl.semaphore_wait(barrier, PLANE + ny + nz - 3)
-
-    def exchange(count, peer, me, source, target, send, recv):
-        def copy(step, mine):
-            other, device = peer(step)
-            return pltpu.make_async_remote_copy(
-                src_ref=source(other),
-                dst_ref=target.at[me if mine else other],
-                send_sem=send.at[other],
-                recv_sem=recv.at[me if mine else other],
-                device_id=device,
-                device_id_type=MESH,
-            )
-
-        def start(step, carry):
-            copy(step, True).start()
-            return carry
-
-        def finish(step, carry):
-            copy(step, True).wait_send()
-            copy(step, False).wait_recv()
-            return carry
-
-        lax.fori_loop(1, count, start, 0)
-        lax.fori_loop(1, count, finish, 0)
-
+    greet_all(((PLANE, peer_w), (ny, peer_y), (nz, peer_z)))
     exchange(PLANE, peer_w, w, lambda other: local.at[other], parts_w, sw, rw)
     parts_w[w] = local[w]
     stage[0] = jnp.sum(parts_w[...], axis=0)
@@ -398,6 +445,51 @@
     stage[2] = jnp.sum(parts_z[...], axis=0)
     exchange(PLANE, peer_w, w, lambda other: stage.at[2], out, sa, ra)
     out[w] = stage[2]
+
+
+def request_body(nz, wanted, got, parts, sw, rw, sz, rz):
+    row = lax.axis_index("rows")
+    y = lax.axis_index("grp")
+    w = row % PLANE
+    z = row // PLANE
+
+    def peer_w(step):
+        other = (w + step) % PLANE
+        return other, (z * PLANE + other, y)
+
+    def peer_z(step):
+        other = (z + step) % nz
+        return other, (other * PLANE + w, y)
+
+    greet_all(((PLANE, peer_w), (nz, peer_z)))
+    exchange(PLANE, peer_w, w, lambda other: wanted.at[other], parts, sw, rw)
+    parts[w] = wanted[w]
+    exchange(nz, peer_z, z, lambda other: parts, got, sz, rz)
+    got[z] = parts[...]
+
+
+def swap_requests(wanted):
+    nrows = wanted.shape[0]
+    nz = nrows // PLANE
+    dma = pltpu.SemaphoreType.DMA
+    sent = jnp.pad(wanted.reshape(nz, PLANE).T, ((0, 0), (0, 128 - nz)))[:, None, :]
+    got = pl.pallas_call(
+        functools.partial(request_body, nz),
+        out_shape=jax.ShapeDtypeStruct((nz,) + sent.shape, sent.dtype),
+        in_specs=[VMEM],
+        out_specs=VMEM,
+        scratch_shapes=[
+            pltpu.VMEM(sent.shape, sent.dtype),
+            dma((PLANE,)),
+            dma((PLANE,)),
+            dma((nz,)),
+            dma((nz,)),
+        ],
+        compiler_params=pltpu.CompilerParams(collective_id=1, has_side_effects=True),
+        name="swap_requests",
+    )(sent)
+    z = lax.axis_index("rows") // PLANE
+    return lax.dynamic_index_in_dim(got, z, axis=3, keepdims=False).reshape(nrows)
 
 
 def total_gram(gram):
@@ -432,12 +524,6 @@
     return out.reshape(columns, columns)
 
 
-def lower_inverse_of(gram, total_rows):
-    lower = jnp.linalg.cholesky(total_gram(gram) / total_rows)
-    identity = jnp.eye(gram.shape[0], dtype=jnp.float32)
-    return lax.linalg.triangular_solve(lower, identity, left_side=True, lower=True)
-
-
 def exchange_tiles(tiles, requested, owner):
     sent = jnp.take(tiles, requested, axis=0, mode="clip")
     got = lax.all_to_all(sent, "rows", split_axis=0, concat_axis=0, tiled=True)
@@ -459,35 +545,33 @@
     owner = far_tiles // tiles
     hits = owner[:, None] == jnp.arange(nrows, dtype=jnp.int32)[None, :]
     wanted = jnp.sum(jnp.where(hits, (far_tiles % tiles)[:, None], 0), axis=0)
-    requested = lax.all_to_all(wanted, "rows", split_axis=0, concat_axis=0, tiled=True)
+    requested = swap_requests(wanted)
     table = (lists - device_index * tiles).reshape(-1)
 
-    far_side = exchange_tiles(own_side, requested, owner).astype(jnp.float32)
-    far_rows = exchange_tiles(own_rows, requested, owner)
+    far = exchange_tiles(jnp.concatenate([own_rows, own_side], axis=1), requested, owner)
     side = own_side.astype(jnp.float32)
     own_band, own_prior = side[:, 0:1, :], side[:, 1:2, :]
-    far_band, far_prior = far_side[:, 0:1, :], far_side[:, 1:2, :]
     directions = projection.T
     near_half, near_density, norms = near_kernel(table, counts[0], own_rows, own_band, slots)
     far_half, own_inverse = far_kernel(
-        counts[0], own_rows, own_band, far_rows, far_band, norms, near_density, slots
+        counts[0], own_rows, own_band, far, norms, near_density, slots
     )
     far_inverse = exchange_tiles(own_inverse.astype(jnp.bfloat16), requested, owner)
     far_inverse = far_inverse.astype(jnp.float32)
     near_part = near_walk(table, own_rows, own_prior, own_inverse, directions, near_half, slots)
     raw, raw_half, degree, gram = far_walk(
-        far_rows, far_prior, far_inverse, directions, far_half, near_part
-    )
+        far, far_inverse, directions, far_half, near_part
+    )
+    gram, raw_half = lax.optimization_barrier((total_gram(gram), raw_half))
     far_raw = exchange_tiles(raw_half, requested, owner)
     total_rows = nrows * lax.axis_size("grp") * tiles * size
-    lower_inverse = lower_inverse_of(gram, total_rows)
-    basis, near_second = near_apply(table, lower_inverse, raw, own_inverse, near_half, slots)
+    basis, near_second, lower_inverse = near_apply(
+        table, gram, raw, own_inverse, near_half, slots, total_rows
+    )
     second_raw, second_gram = far_apply(
         lower_inverse, far_raw, far_inverse, degree, far_half, near_second
     )
-    embedding = jnp.dot(
-        lower_inverse_of(second_gram, total_rows), second_raw, precision=lax.Precision.HIGHEST
-    )
+    embedding = finish(total_gram(second_gram), second_raw, total_rows)
     return basis[None], embedding[None]
 
 

time: 495 us -> 474 us (0.958)
  waiting for transfers between devices: 203 us -> 274 us
  Pallas kernels: 180 us -> 138 us
  other arithmetic: 31.3 us -> 2.1 us
  starting transfers between devices: 55.2 us -> 35.8 us
    all_to_all x4 -> x3, waiting for transfers between devices: 189 us -> 274 us  [exchange_tiles(): got = lax.all_to_all(sent, 'rows', split_axis=0, concat_axis=0, tiled=True)]
    pallas_call x2, Pallas kernels: 138 us -> 56 us  [total_gram(): pl.pallas_call(functools.partial(reduce_body, nz, ny), out_shape=jax.Shap...]
    pallas_call x1 -> x3, Pallas kernels: 7 us -> 46.6 us  [the longest x1 26.6 us: swap_requests(): pl.pallas_call(functools.partial(request_body, nz), out_shape=jax.ShapeDt...]
    another operation x11 -> x0, other arithmetic: 24.9 us -> none  [the longest x6 13 us: lower_inverse_of(): lower = jnp.linalg.cholesky(total_gram(gram) / total_rows)]
    all_to_all x1 -> x0, starting transfers between devices: 20.4 us -> none  [shards(): lax.all_to_all(wanted, 'rows', split_axis=0, concat_axis=0, tiled=True)]
    all_to_all x1 -> x0, waiting for transfers between devices: 14.1 us -> none  [shards(): lax.all_to_all(wanted, 'rows', split_axis=0, concat_axis=0, tiled=True)]
    all_to_all x4 -> x3, starting transfers between devices: 34.8 us -> 35.8 us  [exchange_tiles(): got = lax.all_to_all(sent, 'rows', split_axis=0, concat_axis=0, tiled=True)]
  transfers between devices with their start and end apart: 5 -> 3, of which waited for: 4 -> 3; matrix products, arithmetic and copies ran while one was open for 4% -> 0% of each run, Pallas kernels for 27% -> 7%
where the time goes in v4:
time: 474 us; the launch traced here: 473 us
  waiting for transfers between devices  274 us (58%)
  Pallas kernels  138 us (29%)
  starting transfers between devices  35.8 us (8%)
  local copies, waits for them, and re-layouts  21.2 us (4%)
    all_to_all x3, waiting for transfers between devices, exchange_tiles(): got = lax.all_to_all(sent, 'rows', split_axis=0, concat_axis=0, tiled=True)  274 us
    pallas_call x2, Pallas kernels, total_gram(): pl.pallas_call(functools.partial(reduce_body, nz, ny), out_shape=jax.Shap...  56 us
    all_to_all x3, starting transfers between devices, exchange_tiles(): got = lax.all_to_all(sent, 'rows', split_axis=0, concat_axis=0, tiled=True)  35.8 us
    pallas_call x1, Pallas kernels, swap_requests(): pl.pallas_call(functools.partial(request_body, nz), out_shape=jax.ShapeDt...  26.6 us
    pallas_call x1, Pallas kernels, near_apply(): pl.pallas_call(functools.partial(near_apply_body, tiles, slots, total_row...  12.4 us
    pallas_call x1, Pallas kernels, near_kernel(): pl.pallas_call(functools.partial(near_kernel_body, tiles, slots), out_sha...  10.8 us
  transfers between devices with their start and end apart: 3, of which 3 were waited for; matrix products, arithmetic and copies ran while one was open for 0% of the time, Pallas kernels for 7%

profile of v4, /device:TPU:1, one launch (start us, length us, event | category | flops | bytes accessed | tf_op | source)
XLA Modules:
  0.0 472.6 jit_solution(14748506847820932069)
XLA Ops:
  0.6 0.7 copy.23
  1.3 0.1 slice_divide_fusion
  1.4 0.1 compare_and_fusion
  1.5 0.1 div.29
  1.6 0.1 ne.64
  1.7 0.1 rem.45
  1.8 0.1 select_reduce_fusion
  1.9 0.1 reshape.105
  2.0 0.1 copy.14
  2.0 0.6 pad.4
  2.7 26.6 %swap_requests.1 = s32[16,8,1,128]{3,2,1,0:T(1,128)} custom-call(s32[8,1,128]{2,1,0:T(1,128)} %bitcast.46), custom_call_target="tpu_custom_call" | custom-call | tf_op jit(solution)/shard_map/swap_requests/pallas_call | solution.py:476
  29.3 3.3 dynamic-slice_reduce_fusion
  32.6 0.1 reshape.112
  32.7 1.1 pad_maximum_fusion
  33.8 3.3 gather_fusion
  37.1 0.0 copy-start.2
  37.1 0.0 copy-start
  37.1 0.0 copy-start.1
  37.1 13.7 %all-to-all-start = ((bf16[128,130,128]{2,1,0:T(8,128)(2,1)}), bf16[128,130,128]{2,1,0:T(8,128)(2,1)}, u32[]{:S(2)}, u32[]{:S(2)}) async-start(bf16[128,130,128]{2,1,0:T(8,128)(2,1)} %gather_fusion), calls=%async_computation | async-start | bytes 8912896 | tf_op jit(solution)/shard_map/all_to_all | solution.py:529
  50.8 0.1 div.33
  50.9 0.0 copy-done.2
  50.9 0.6 sub.24.table
  51.6 0.1 and.35
  51.6 0.0 copy-done
  51.7 0.0 copy-done.1
  51.7 0.6 fusion.1
  52.3 10.8 %near_kernel.1 = (bf16[12,13,128,128]{3,2,1,0:T(8,128)(2,1)}, f32[12,1,128]{2,1,0:T(1,128)}, f32[12,1,128]{2,1,0:T(1,128)}) custom-call(s32[192]{0:T(256)} %sub.24.table, s32[12]{0:T(128)} %bitcast.47, bf16[12,128,128]{2,1,0:T(8,128)(2,1)} %bitcast.27, f32[12,1,128]{2,1,0:T(1,128)} %get-tuple-element.37.band), custom_call_target="tpu_custom_call" | custom-call | flops 1022361600 | bytes 10223616 | tf_op jit(solution)/shard_map/near_kernel/pallas_call | solution.py:83
  63.1 183.0 %all-to-all-done = bf16[128,130,128]{2,1,0:T(8,128)(2,1)} async-done(((bf16[128,130,128]{2,1,0:T(8,128)(2,1)}), bf16[128,130,128]{2,1,0:T(8,128)(2,1)}, u32[]{:S(2)}, u32[]{:S(2)}) %all-to-all-start) | async-done | bytes 4259872 | tf_op jit(solution)/shard_map/all_to_all | solution.py:529
  246.1 4.2 gather_fusion.1
  250.3 4.8 %far_kernel.1 = (bf16[12,3,128,128]{3,2,1,0:T(8,128)(2,1)}, f32[12,1,128]{2,1,0:T(1,128)}) custom-call(s32[12]{0:T(128)} %bitcast.48, bf16[12,128,128]{2,1,0:T(8,128)(2,1)} %bitcast.28, f32[12,1,128]{2,1,0:T(1,128)} %get-tuple-element.37.band, bf16[36,130,128]{2,1,0:T(8,128)(2,1)} %gather_fusion.1, f32[12,1,128]{2,1,0:T(1,128)} %get-tuple-element.18.norm_a, ...), custom_call_target="tpu_custom_call" | custom-call | tf_op jit(solution)/shard_map/far_kernel/pallas_call | solution.py:128
  255.1 0.7 convert_element_type.10
  255.8 0.7 gather_fusion.2
  256.5 0.7 copy.15
  257.2 12.6 %all-to-all-start.1 = ((bf16[128,1,128]{2,1,0:T(2,128)(2,1)}), bf16[128,1,128]{2,1,0:T(2,128)(2,1)S(1)}, u32[]{:S(2)}, u32[]{:S(2)}) async-start(bf16[128,1,128]{2,1,0:T(2,128)(2,1)} %copy.15), calls=%async_computation.1 | async-start | bytes 131072 | tf_op jit(solution)/shard_map/all_to_all | solution.py:529
  269.8 8.0 %near_walk.1.partial = f32[12,80,128]{2,1,0:T(8,128)} custom-call(s32[192]{0:T(256)} %sub.24.table, bf16[12,128,128]{2,1,0:T(8,128)(2,1)} %bitcast.29, f32[12,1,128]{2,1,0:T(1,128)} %get-tuple-element.36.prior, f32[12,1,128]{2,1,0:T(1,128)} %get-tuple-element.20.inverse, bf16[64,128]{1,0:T(8,128)(2,1)} %bitcast.37, ...), custom_call_target="tpu_custom_call" | custom-call | flops 408944640 | bytes 10223616 | tf_op jit(solution)/shard_map/near_walk/pallas_call | solution.py:183
  277.8 6.8 %all-to-all-done.1 = bf16[128,1,128]{2,1,0:T(2,128)(2,1)S(1)} async-done(((bf16[128,1,128]{2,1,0:T(2,128)(2,1)}), bf16[128,1,128]{2,1,0:T(2,128)(2,1)S(1)}, u32[]{:S(2)}, u32[]{:S(2)}) %all-to-all-start.1) | async-done | bytes 32800 | tf_op jit(solution)/shard_map/all_to_all | solution.py:529
  284.6 0.6 gather_fusion.3
  285.2 0.6 reshape.162.inverse
  285.8 6.1 %far_walk.1 = (f32[64,1536]{1,0:T(8,128)}, bf16[12,64,128]{2,1,0:T(8,128)(2,1)}, f32[12,1,128]{2,1,0:T(1,128)}, f32[64,64]{1,0:T(8,128)}) custom-call(bf16[36,130,128]{2,1,0:T(8,128)(2,1)} %gather_fusion.1, f32[36,1,128]{2,1,0:T(1,128)} %reshape.162.inverse, bf16[64,128]{1,0:T(8,128)(2,1)} %bitcast.38, ...), custom_call_target="tpu_custom_call" | custom-call | tf_op jit(solution)/shard_map/far_walk/pallas_call | solution.py:237
  292.0 27.8 %gram_reduce.2 = f32[8,8,64]{2,1,0:T(8,128)} custom-call(f32[8,8,64]{2,1,0:T(8,128)} %bitcast.40), custom_call_target="tpu_custom_call" | custom-call | tf_op jit(solution)/shard_map/gram_reduce/pallas_call | solution.py:502
  319.8 3.1 gather_fusion.4
  322.9 9.5 %all-to-all-start.2 = ((bf16[128,64,128]{2,1,0:T(8,128)(2,1)}), bf16[128,64,128]{2,1,0:T(8,128)(2,1)S(1)}, u32[]{:S(2)}, u32[]{:S(2)}) async-start(bf16[128,64,128]{2,1,0:T(8,128)(2,1)} %gather_fusion.4), calls=%async_computation.2 | async-start | bytes 4194304 | tf_op jit(solution)/shard_map/all_to_all | solution.py:529
  332.4 12.4 %near_apply.1 = (f32[64,1536]{1,0:T(8,128)}, f32[12,64,128]{2,1,0:T(8,128)}, f32[64,64]{1,0:T(8,128)}) custom-call(s32[192]{0:T(256)} %sub.24.table, f32[64,64]{1,0:T(8,128)} %bitcast.32, f32[64,1536]{1,0:T(8,128)} %get-tuple-element.26.raw, f32[12,1,128]{2,1,0:T(1,128)} %get-tuple-element.20.inverse, bf16[12,13,128,128]{3,2,1,0:T(8,128)(2,1)} %get-tuple-element.22.kernel_half), custom_call_target="tpu_custom_call" | custom-call | flops 327155712 | bytes 10223616 | tf_op jit(solution)/shard_map/near_apply/pallas_call | solution.py:319
  344.8 84.5 %all-to-all-done.2 = bf16[128,64,128]{2,1,0:T(8,128)(2,1)S(1)} async-done(((bf16[128,64,128]{2,1,0:T(8,128)(2,1)}), bf16[128,64,128]{2,1,0:T(8,128)(2,1)S(1)}, u32[]{:S(2)}, u32[]{:S(2)}) %all-to-all-start.2) | async-done | bytes 2097184 | tf_op jit(solution)/shard_map/all_to_all | solution.py:529
  429.3 1.5 gather_fusion.5
  430.8 6.0 %far_apply.1 = (f32[64,1536]{1,0:T(8,128)}, f32[64,64]{1,0:T(8,128)}) custom-call(f32[64,64]{1,0:T(8,128)} %get-tuple-element.28.lower_inverse, bf16[36,64,128]{2,1,0:T(8,128)(2,1)} %gather_fusion.5, f32[36,1,128]{2,1,0:T(1,128)} %reshape.162.inverse, f32[12,1,128]{2,1,0:T(1,128)} %get-tuple-element.30.degree, ...), custom_call_target="tpu_custom_call" | custom-call | tf_op jit(solution)/shard_map/far_apply/pallas_call | solution.py:367
  436.8 28.2 %gram_reduce.3 = f32[8,8,64]{2,1,0:T(8,128)} custom-call(f32[8,8,64]{2,1,0:T(8,128)} %bitcast.39), custom_call_target="tpu_custom_call" | custom-call | tf_op jit(solution)/shard_map/gram_reduce/pallas_call | solution.py:502
  465.0 7.6 %finish.1 = f32[64,1536]{1,0:T(8,128)} custom-call(f32[64,64]{1,0:T(8,128)} %bitcast.34, f32[64,1536]{1,0:T(8,128)} %get-tuple-element.33.raw), custom_call_target="tpu_custom_call" | custom-call | tf_op jit(solution)/shard_map/finish/pallas_call | solution.py:277
  (8 shorter events, 0.1 us)
Async XLA Ops:
  37.1 13.8 %copy-start.2 = (s32[1,12,16]{2,0,1:T(1,128)S(1)}, s32[1,12,16]{2,0,1:T(1,128)}, u32[]{:S(2)}) copy-start(s32[1,12,16]{2,0,1:T(1,128)} %param.9) | copy-start | bytes 2308
  37.1 14.5 %copy-start = (bf16[1,1536]{1,0:T(2,128)(2,1)S(1)}, bf16[1,1536]{1,0:T(2,128)(2,1)}, u32[]{:S(2)}) copy-start(bf16[1,1536]{1,0:T(2,128)(2,1)} %param.8) | copy-start | bytes 9220
  37.1 14.5 %copy-start.1 = (bf16[1,1536]{1,0:T(2,128)(2,1)S(1)}, bf16[1,1536]{1,0:T(2,128)(2,1)}, u32[]{:S(2)}) copy-start(bf16[1,1536]{1,0:T(2,128)(2,1)} %param.7) | copy-start | bytes 9220
  37.1 209.0 %all-to-all-start = ((bf16[128,130,128]{2,1,0:T(8,128)(2,1)}), bf16[128,130,128]{2,1,0:T(8,128)(2,1)}, u32[]{:S(2)}, u32[]{:S(2)}) async-start(bf16[128,130,128]{2,1,0:T(8,128)(2,1)} %gather_fusion), calls=%async_computation | async-start | bytes 8912896 | tf_op jit(solution)/shard_map/all_to_all | solution.py:529
  257.2 27.4 %all-to-all-start.1 = ((bf16[128,1,128]{2,1,0:T(2,128)(2,1)}), bf16[128,1,128]{2,1,0:T(2,128)(2,1)S(1)}, u32[]{:S(2)}, u32[]{:S(2)}) async-start(bf16[128,1,128]{2,1,0:T(2,128)(2,1)} %copy.15), calls=%async_computation.1 | async-start | bytes 131072 | tf_op jit(solution)/shard_map/all_to_all | solution.py:529
  322.9 106.4 %all-to-all-start.2 = ((bf16[128,64,128]{2,1,0:T(8,128)(2,1)}), bf16[128,64,128]{2,1,0:T(8,128)(2,1)S(1)}, u32[]{:S(2)}, u32[]{:S(2)}) async-start(bf16[128,64,128]{2,1,0:T(8,128)(2,1)} %gather_fusion.4), calls=%async_computation.2 | async-start | bytes 4194304 | tf_op jit(solution)/shard_map/all_to_all | solution.py:529

commit v5 on v4

--- a/solution.py
+++ b/solution.py
@@ -415,36 +415,66 @@
     pl.semaphore_wait(barrier, sum(count - 1 for count, _ in groups))
 
 
-def reduce_body(nz, ny, local, out, parts_w, parts_y, parts_z, stage, sw, rw, sy, ry, sz, rz, sa, ra):
+def reduce_body(nz, ny, local, total, chunks, parts, parts_z, sums, gathered, sp, rp, sz, rz, sa, ra):
     row = lax.axis_index("rows")
     y = lax.axis_index("grp")
     w = row % PLANE
     z = row // PLANE
-
-    def peer_w(step):
-        other = (w + step) % PLANE
-        return other, (z * PLANE + other, y)
-
-    def peer_y(step):
-        other = (y + step) % ny
-        return other, (row, other)
+    count = PLANE * ny
+    me = y * PLANE + w
+    height = local.shape[0] // count
+
+    def peer_p(step):
+        other = (me + step) % count
+        return other, (z * PLANE + other % PLANE, other // PLANE)
 
     def peer_z(step):
         other = (z + step) % nz
         return other, (other * PLANE + w, y)
 
-    greet_all(((PLANE, peer_w), (ny, peer_y), (nz, peer_z)))
-    exchange(PLANE, peer_w, w, lambda other: local.at[other], parts_w, sw, rw)
-    parts_w[w] = local[w]
-    stage[0] = jnp.sum(parts_w[...], axis=0)
-    exchange(ny, peer_y, y, lambda other: stage.at[0], parts_y, sy, ry)
-    parts_y[y] = stage[0]
-    stage[1] = jnp.sum(parts_y[...], axis=0)
-    exchange(nz, peer_z, z, lambda other: stage.at[1], parts_z, sz, rz)
-    parts_z[z] = stage[1]
-    stage[2] = jnp.sum(parts_z[...], axis=0)
-    exchange(PLANE, peer_w, w, lambda other: stage.at[2], out, sa, ra)
-    out[w] = stage[2]
+    for index in range(count):
+        chunks[index] = local[index * height : (index + 1) * height, :]
+    greet_all(((count, peer_p), (nz, peer_z)))
+    exchange(count, peer_p, me, lambda other: chunks.at[other], parts, sp, rp)
+    parts[me] = chunks[me]
+    sums[0] = jnp.sum(parts[...], axis=0)
+    exchange(nz, peer_z, z, lambda other: sums.at[0], parts_z, sz, rz)
+    parts_z[z] = sums[0]
+    sums[1] = jnp.sum(parts_z[...], axis=0)
+    exchange(count, peer_p, me, lambda other: sums.at[1], gathered, sa, ra)
+    gathered[me] = sums[1]
+    for index in range(count):
+        total[index * height : (index + 1) * height, :] = gathered[index]
+
+
+def total_gram(gram):
+    columns = gram.shape[0]
+    ny = lax.axis_size("grp")
+    nz = lax.axis_size("rows") // PLANE
+    count = PLANE * ny
+    chunk = (columns // count, columns)
+    dma = pltpu.SemaphoreType.DMA
+    return pl.pallas_call(
+        functools.partial(reduce_body, nz, ny),
+        out_shape=jax.ShapeDtypeStruct(gram.shape, jnp.float32),
+        in_specs=[VMEM],
+        out_specs=VMEM,
+        scratch_shapes=[
+            pltpu.VMEM((count,) + chunk, jnp.float32),
+            pltpu.VMEM((count,) + chunk, jnp.float32),
+            pltpu.VMEM((nz,) + chunk, jnp.float32),
+            pltpu.VMEM((2,) + chunk, jnp.float32),
+            pltpu.VMEM((count,) + chunk, jnp.float32),
+            dma((count,)),
+            dma((count,)),
+            dma((nz,)),
+            dma((nz,)),
+            dma((count,)),
+            dma((count,)),
+        ],
+        compiler_params=pltpu.CompilerParams(collective_id=0, has_side_effects=True),
+        name="gram_reduce",
+    )(gram)
 
 
 def request_body(nz, wanted, got, parts, sw, rw, sz, rz):
@@ -492,38 +522,6 @@
     return lax.dynamic_index_in_dim(got, z, axis=3, keepdims=False).reshape(nrows)
 
 
-def total_gram(gram):
-    columns = gram.shape[0]
-    height = columns // PLANE
-    ny = lax.axis_size("grp")
-    nz = lax.axis_size("rows") // PLANE
-    chunk = (height, columns)
-    dma = pltpu.SemaphoreType.DMA
-    out = pl.pallas_call(
-        functools.partial(reduce_body, nz, ny),
-        out_shape=jax.ShapeDtypeStruct((PLANE,) + chunk, jnp.float32),
-        in_specs=[VMEM],
-        out_specs=VMEM,
-        scratch_shapes=[
-            pltpu.VMEM((PLANE,) + chunk, jnp.float32),
-            pltpu.VMEM((ny,) + chunk, jnp.float32),
-            pltpu.VMEM((nz,) + chunk, jnp.float32),
-            pltpu.VMEM((3,) + chunk, jnp.float32),
-            dma((PLANE,)),
-            dma((PLANE,)),
-            dma((ny,)),
-            dma((ny,)),
-            dma((nz,)),
-            dma((nz,)),
-            dma((PLANE,)),
-            dma((PLANE,)),
-        ],
-        compiler_params=pltpu.CompilerParams(collective_id=0, has_side_effects=True),
-        name="gram_reduce",
-    )(gram.reshape((PLANE,) + chunk))
-    return out.reshape(columns, columns)
-
-
 def exchange_tiles(tiles, requested, owner):
     sent = jnp.take(tiles, requested, axis=0, mode="clip")
     got = lax.all_to_all(sent, "rows", split_axis=0, concat_axis=0, tiled=True)
@@ -548,7 +546,8 @@
     requested = swap_requests(wanted)
     table = (lists - device_index * tiles).reshape(-1)
 
-    far = exchange_tiles(jnp.concatenate([own_rows, own_side], axis=1), requested, owner)
+    packed = jnp.concatenate([own_rows, own_side], axis=1).reshape(tiles, 2, -1)
+    far = exchange_tiles(packed, requested, owner).reshape(owner.shape[0], size + 2, -1)
     side = own_side.astype(jnp.float32)
     own_band, own_prior = side[:, 0:1, :], side[:, 1:2, :]
     directions = projection.T

time: 474 us -> 482 us (1.017)
  local copies, waits for them, and re-layouts: 21.2 us -> 37.3 us
  waiting for transfers between devices: 274 us -> 265 us
    all_to_all x3, waiting for transfers between devices: 274 us -> 265 us  [exchange_tiles(): got = lax.all_to_all(sent, 'rows', split_axis=0, concat_axis=0, tiled=True)]
    gather x4, local copies, waits for them, and re-layouts: 7.82 us -> 16.4 us  [exchange_tiles(): sent = jnp.take(tiles, requested, axis=0, mode='clip')]
  transfers between devices with their start and end apart: 3 -> 3, of which waited for: 3 -> 3; matrix products, arithmetic and copies ran while one was open for 0% -> 0% of each run, Pallas kernels for 7% -> 6%
where the time goes in v5:
time: 482 us; the launch traced here: 481 us
  waiting for transfers between devices  265 us (55%)
  Pallas kernels  140 us (29%)
  local copies, waits for them, and re-layouts  37.3 us (8%)
  starting transfers between devices  36.1 us (7%)
    all_to_all x3, waiting for transfers between devices, exchange_tiles(): got = lax.all_to_all(sent, 'rows', split_axis=0, concat_axis=0, tiled=True)  265 us
    pallas_call x2, Pallas kernels, total_gram(): pl.pallas_call(functools.partial(reduce_body, nz, ny), out_shape=jax.Shap...  57.3 us
    all_to_all x3, starting transfers between devices, exchange_tiles(): got = lax.all_to_all(sent, 'rows', split_axis=0, concat_axis=0, tiled=True)  36.1 us
    pallas_call x1, Pallas kernels, swap_requests(): pl.pallas_call(functools.partial(request_body, nz), out_shape=jax.ShapeDt...  26.6 us
    gather x4, local copies, waits for them, and re-layouts, exchange_tiles(): sent = jnp.take(tiles, requested, axis=0, mode='clip')  16.4 us
    pallas_call x1, Pallas kernels, near_apply(): pl.pallas_call(functools.partial(near_apply_body, tiles, slots, total_row...  12.4 us
    pallas_call x1, Pallas kernels, near_kernel(): pl.pallas_call(functools.partial(near_kernel_body, tiles, slots), out_sha...  10.8 us
    gather x3, local copies, waits for them, and re-layouts, exchange_tiles(): return jnp.take(got, owner, axis=0, mode='clip')  10.6 us
  transfers between devices with their start and end apart: 3, of which 3 were waited for; matrix products, arithmetic and copies ran while one was open for 0% of the time, Pallas kernels for 6%

profile of v5, /device:TPU:1, one launch (start us, length us, event | category | flops | bytes accessed | tf_op | source)
XLA Modules:
  0.0 481.3 jit_solution(680551682702952476)
XLA Ops:
  0.6 0.7 copy.23
  1.3 0.1 compare_and_fusion
  1.4 0.1 slice_divide_fusion
  1.5 0.1 ne.64
  1.6 0.1 rem.45
  1.7 0.1 div.29
  1.8 0.1 select_reduce_fusion
  1.9 0.1 reshape.100
  2.0 0.1 copy.14
  2.0 0.6 pad.4
  2.6 26.6 %swap_requests.1 = s32[16,8,1,128]{3,2,1,0:T(1,128)} custom-call(s32[8,1,128]{2,1,0:T(1,128)} %bitcast.38), custom_call_target="tpu_custom_call" | custom-call | tf_op jit(solution)/shard_map/swap_requests/pallas_call | solution.py:506
  29.3 3.3 dynamic-slice_reduce_fusion
  32.6 0.1 reshape.104
  32.7 1.1 pad_maximum_fusion
  33.8 0.1 reshape.99
  33.9 11.9 %gather_fusion = bf16[128,2,8320]{2,1,0:T(2,128)(2,1)} fusion(bf16[12,2,8320]{2,1,0:T(2,128)(2,1)S(1)} %reshape.99, s32[1024]{0:T(1024)S(1)} %pad_clamp_fusion.1), kind=kCustom, calls=%fused_computation | custom fusion | bytes 8520192 | tf_op jit(solution)/shard_map/jit(_take)/gather | solution.py:526
  45.8 0.0 copy-start.2
  45.8 13.8 %all-to-all-start = ((bf16[128,2,8320]{2,1,0:T(2,128)(2,1)}), bf16[128,2,8320]{2,1,0:T(2,128)(2,1)}, u32[]{:S(2)}, u32[]{:S(2)}) async-start(bf16[128,2,8320]{2,1,0:T(2,128)(2,1)} %gather_fusion), calls=%async_computation | async-start | bytes 8519680 | tf_op jit(solution)/shard_map/all_to_all | solution.py:527
  59.6 0.1 div.33
  59.7 0.0 copy-done.2
  59.7 0.7 sub.24.table
  60.4 0.1 and.35
  60.5 0.0 copy-done
  60.5 0.0 copy-done.1
  60.5 0.6 fusion.1
  61.1 10.8 %near_kernel.1 = (bf16[12,13,128,128]{3,2,1,0:T(8,128)(2,1)}, f32[12,1,128]{2,1,0:T(1,128)}, f32[12,1,128]{2,1,0:T(1,128)}) custom-call(s32[192]{0:T(256)} %sub.24.table, s32[12]{0:T(128)} %bitcast.39, bf16[12,128,128]{2,1,0:T(8,128)(2,1)} %bitcast.23, f32[12,1,128]{2,1,0:T(1,128)} %get-tuple-element.37.band), custom_call_target="tpu_custom_call" | custom-call | flops 1022361600 | bytes 10223616 | tf_op jit(solution)/shard_map/near_kernel/pallas_call | solution.py:83
  72.0 174.1 %all-to-all-done = bf16[128,2,8320]{2,1,0:T(2,128)(2,1)} async-done(((bf16[128,2,8320]{2,1,0:T(2,128)(2,1)}), bf16[128,2,8320]{2,1,0:T(2,128)(2,1)}, u32[]{:S(2)}, u32[]{:S(2)}) %all-to-all-start) | async-done | bytes 4259872 | tf_op jit(solution)/shard_map/all_to_all | solution.py:527
  246.1 8.5 %gather_fusion.1 = bf16[36,2,8320]{2,1,0:T(2,128)(2,1)S(1)} fusion(bf16[128,2,8320]{2,1,0:T(2,128)(2,1)} %all-to-all-done, s32[1024]{0:T(1024)S(1)} %pad_clamp_fusion), kind=kCustom, calls=%fused_computation.1 | custom fusion | bytes 2396304 | tf_op jit(solution)/shard_map/jit(_take)/gather | solution.py:528
  254.6 2.9 reshape.101.far
  257.5 4.8 %far_kernel.1 = (bf16[12,3,128,128]{3,2,1,0:T(8,128)(2,1)}, f32[12,1,128]{2,1,0:T(1,128)}) custom-call(s32[12]{0:T(128)} %bitcast.40, bf16[12,128,128]{2,1,0:T(8,128)(2,1)} %bitcast.24, f32[12,1,128]{2,1,0:T(1,128)} %get-tuple-element.37.band, bf16[36,130,128]{2,1,0:T(8,128)(2,1)} %reshape.101.far, f32[12,1,128]{2,1,0:T(1,128)} %get-tuple-element.18.norm_a, ...), custom_call_target="tpu_custom_call" | custom-call | tf_op jit(solution)/shard_map/far_kernel/pallas_call | solution.py:128
  262.4 0.7 convert_element_type.10
  263.1 0.7 gather_fusion.2
  263.8 0.7 copy.15
  264.5 13.0 %all-to-all-start.1 = ((bf16[128,1,128]{2,1,0:T(2,128)(2,1)}), bf16[128,1,128]{2,1,0:T(2,128)(2,1)S(1)}, u32[]{:S(2)}, u32[]{:S(2)}) async-start(bf16[128,1,128]{2,1,0:T(2,128)(2,1)} %copy.15), calls=%async_computation.1 | async-start | bytes 131072 | tf_op jit(solution)/shard_map/all_to_all | solution.py:527
  277.5 8.0 %near_walk.1.partial = f32[12,80,128]{2,1,0:T(8,128)} custom-call(s32[192]{0:T(256)} %sub.24.table, bf16[12,128,128]{2,1,0:T(8,128)(2,1)} %bitcast.25, f32[12,1,128]{2,1,0:T(1,128)} %get-tuple-element.36.prior, f32[12,1,128]{2,1,0:T(1,128)} %get-tuple-element.20.inverse, bf16[64,128]{1,0:T(8,128)(2,1)} %bitcast.31, ...), custom_call_target="tpu_custom_call" | custom-call | flops 408944640 | bytes 10223616 | tf_op jit(solution)/shard_map/near_walk/pallas_call | solution.py:183
  285.5 6.8 %all-to-all-done.1 = bf16[128,1,128]{2,1,0:T(2,128)(2,1)S(1)} async-done(((bf16[128,1,128]{2,1,0:T(2,128)(2,1)}), bf16[128,1,128]{2,1,0:T(2,128)(2,1)S(1)}, u32[]{:S(2)}, u32[]{:S(2)}) %all-to-all-start.1) | async-done | bytes 32800 | tf_op jit(solution)/shard_map/all_to_all | solution.py:527
  292.3 0.6 gather_fusion.3
  292.9 0.6 reshape.154.inverse
  293.5 6.1 %far_walk.1 = (f32[64,1536]{1,0:T(8,128)}, bf16[12,64,128]{2,1,0:T(8,128)(2,1)}, f32[12,1,128]{2,1,0:T(1,128)}, f32[64,64]{1,0:T(8,128)}) custom-call(bf16[36,130,128]{2,1,0:T(8,128)(2,1)} %reshape.101.far, f32[36,1,128]{2,1,0:T(1,128)} %reshape.154.inverse, bf16[64,128]{1,0:T(8,128)(2,1)} %bitcast.32, ...), custom_call_target="tpu_custom_call" | custom-call | tf_op jit(solution)/shard_map/far_walk/pallas_call | solution.py:237
  299.6 27.7 %gram_reduce.2.gram = f32[64,64]{1,0:T(8,128)} custom-call(f32[64,64]{1,0:T(8,128)} %get-tuple-element.23.local), custom_call_target="tpu_custom_call" | custom-call | tf_op jit(solution)/shard_map/gram_reduce/pallas_call | solution.py:457
  327.4 3.1 gather_fusion.4
  330.5 9.3 %all-to-all-start.2 = ((bf16[128,64,128]{2,1,0:T(8,128)(2,1)}), bf16[128,64,128]{2,1,0:T(8,128)(2,1)S(1)}, u32[]{:S(2)}, u32[]{:S(2)}) async-start(bf16[128,64,128]{2,1,0:T(8,128)(2,1)} %gather_fusion.4), calls=%async_computation.2 | async-start | bytes 4194304 | tf_op jit(solution)/shard_map/all_to_all | solution.py:527
  339.8 12.4 %near_apply.1 = (f32[64,1536]{1,0:T(8,128)}, f32[12,64,128]{2,1,0:T(8,128)}, f32[64,64]{1,0:T(8,128)}) custom-call(s32[192]{0:T(256)} %sub.24.table, f32[64,64]{1,0:T(8,128)} %gram_reduce.2.gram, f32[64,1536]{1,0:T(8,128)} %get-tuple-element.26.raw, f32[12,1,128]{2,1,0:T(1,128)} %get-tuple-element.20.inverse, ...), custom_call_target="tpu_custom_call" | custom-call | flops 327155712 | bytes 10223616 | tf_op jit(solution)/shard_map/near_apply/pallas_call | solution.py:319
  352.2 84.5 %all-to-all-done.2 = bf16[128,64,128]{2,1,0:T(8,128)(2,1)S(1)} async-done(((bf16[128,64,128]{2,1,0:T(8,128)(2,1)}), bf16[128,64,128]{2,1,0:T(8,128)(2,1)S(1)}, u32[]{:S(2)}, u32[]{:S(2)}) %all-to-all-start.2) | async-done | bytes 2097184 | tf_op jit(solution)/shard_map/all_to_all | solution.py:527
  436.7 1.5 gather_fusion.5
  438.2 6.0 %far_apply.1 = (f32[64,1536]{1,0:T(8,128)}, f32[64,64]{1,0:T(8,128)}) custom-call(f32[64,64]{1,0:T(8,128)} %get-tuple-element.28.lower_inverse, bf16[36,64,128]{2,1,0:T(8,128)(2,1)} %gather_fusion.5, f32[36,1,128]{2,1,0:T(1,128)} %reshape.154.inverse, f32[12,1,128]{2,1,0:T(1,128)} %get-tuple-element.30.degree, ...), custom_call_target="tpu_custom_call" | custom-call | tf_op jit(solution)/shard_map/far_apply/pallas_call | solution.py:367
  444.2 29.5 %gram_reduce.3.gram = f32[64,64]{1,0:T(8,128)} custom-call(f32[64,64]{1,0:T(8,128)} %get-tuple-element.32.local), custom_call_target="tpu_custom_call" | custom-call | tf_op jit(solution)/shard_map/gram_reduce/pallas_call | solution.py:457
  473.8 7.6 %finish.1 = f32[64,1536]{1,0:T(8,128)} custom-call(f32[64,64]{1,0:T(8,128)} %gram_reduce.3.gram, f32[64,1536]{1,0:T(8,128)} %get-tuple-element.33.raw), custom_call_target="tpu_custom_call" | custom-call | tf_op jit(solution)/shard_map/finish/pallas_call | solution.py:277
  (10 shorter events, 0.1 us)
Async XLA Ops:
  45.8 13.9 %copy-start.2 = (s32[1,12,16]{2,0,1:T(1,128)S(1)}, s32[1,12,16]{2,0,1:T(1,128)}, u32[]{:S(2)}) copy-start(s32[1,12,16]{2,0,1:T(1,128)} %param.9) | copy-start | bytes 2308
  45.8 14.7 %copy-start = (bf16[1,1536]{1,0:T(2,128)(2,1)S(1)}, bf16[1,1536]{1,0:T(2,128)(2,1)}, u32[]{:S(2)}) copy-start(bf16[1,1536]{1,0:T(2,128)(2,1)} %param.8) | copy-start | bytes 9220
  45.8 14.7 %copy-start.1 = (bf16[1,1536]{1,0:T(2,128)(2,1)S(1)}, bf16[1,1536]{1,0:T(2,128)(2,1)}, u32[]{:S(2)}) copy-start(bf16[1,1536]{1,0:T(2,128)(2,1)} %param.7) | copy-start | bytes 9220
  45.8 200.2 %all-to-all-start = ((bf16[128,2,8320]{2,1,0:T(2,128)(2,1)}), bf16[128,2,8320]{2,1,0:T(2,128)(2,1)}, u32[]{:S(2)}, u32[]{:S(2)}) async-start(bf16[128,2,8320]{2,1,0:T(2,128)(2,1)} %gather_fusion), calls=%async_computation | async-start | bytes 8519680 | tf_op jit(solution)/shard_map/all_to_all | solution.py:527
  264.5 27.8 %all-to-all-start.1 = ((bf16[128,1,128]{2,1,0:T(2,128)(2,1)}), bf16[128,1,128]{2,1,0:T(2,128)(2,1)S(1)}, u32[]{:S(2)}, u32[]{:S(2)}) async-start(bf16[128,1,128]{2,1,0:T(2,128)(2,1)} %copy.15), calls=%async_computation.1 | async-start | bytes 131072 | tf_op jit(solution)/shard_map/all_to_all | solution.py:527
  330.5 106.2 %all-to-all-start.2 = ((bf16[128,64,128]{2,1,0:T(8,128)(2,1)}), bf16[128,64,128]{2,1,0:T(8,128)(2,1)S(1)}, u32[]{:S(2)}, u32[]{:S(2)}) async-start(bf16[128,64,128]{2,1,0:T(8,128)(2,1)} %gather_fusion.4), calls=%async_computation.2 | async-start | bytes 4194304 | tf_op jit(solution)/shard_map/all_to_all | solution.py:527

commit v6 on v4

--- a/solution.py
+++ b/solution.py
@@ -562,8 +562,8 @@
     raw, raw_half, degree, gram = far_walk(
         far, far_inverse, directions, far_half, near_part
     )
-    gram, raw_half = lax.optimization_barrier((total_gram(gram), raw_half))
     far_raw = exchange_tiles(raw_half, requested, owner)
+    gram = total_gram(gram)
     total_rows = nrows * lax.axis_size("grp") * tiles * size
     basis, near_second, lower_inverse = near_apply(
         table, gram, raw, own_inverse, near_half, slots, total_rows

time: 474 us -> 471 us (level)
  waiting for transfers between devices: 274 us -> 190 us
  Pallas kernels: 138 us -> 220 us
    all_to_all x3, waiting for transfers between devices: 274 us -> 190 us  [exchange_tiles(): got = lax.all_to_all(sent, 'rows', split_axis=0, concat_axis=0, tiled=True)]
    pallas_call x2, Pallas kernels: 56 us -> 138 us  [total_gram(): pl.pallas_call(functools.partial(reduce_body, nz, ny), out_shape=jax.Shap...]
  transfers between devices with their start and end apart: 3 -> 3, of which waited for: 3 -> 2; matrix products, arithmetic and copies ran while one was open for 0% -> 0% of each run, Pallas kernels for 7% -> 30%
where the time goes in v6:
time: 471 us; the launch traced here: 470 us
  Pallas kernels  220 us (47%)
  waiting for transfers between devices  190 us (40%)
  starting transfers between devices  35.6 us (8%)
  local copies, waits for them, and re-layouts  21.2 us (5%)
    all_to_all x3, waiting for transfers between devices, exchange_tiles(): got = lax.all_to_all(sent, 'rows', split_axis=0, concat_axis=0, tiled=True)  190 us
    pallas_call x2, Pallas kernels, total_gram(): pl.pallas_call(functools.partial(reduce_body, nz, ny), out_shape=jax.Shap...  138 us
    all_to_all x3, starting transfers between devices, exchange_tiles(): got = lax.all_to_all(sent, 'rows', split_axis=0, concat_axis=0, tiled=True)  35.6 us
    pallas_call x1, Pallas kernels, swap_requests(): pl.pallas_call(functools.partial(request_body, nz), out_shape=jax.ShapeDt...  26.6 us
    pallas_call x1, Pallas kernels, near_apply(): pl.pallas_call(functools.partial(near_apply_body, tiles, slots, total_row...  12.4 us
    pallas_call x1, Pallas kernels, near_kernel(): pl.pallas_call(functools.partial(near_kernel_body, tiles, slots), out_sha...  10.8 us
  transfers between devices with their start and end apart: 3, of which 2 were waited for; matrix products, arithmetic and copies ran while one was open for 0% of the time, Pallas kernels for 30%

profile of v6, /device:TPU:1, one launch (start us, length us, event | category | flops | bytes accessed | tf_op | source)
XLA Modules:
  0.0 469.6 jit_solution(15170281723465522337)
XLA Ops:
  0.6 0.7 copy.23
  1.3 0.1 slice_divide_fusion
  1.4 0.1 compare_and_fusion
  1.5 0.1 div.29
  1.6 0.1 ne.64
  1.7 0.1 rem.45
  1.8 0.1 select_reduce_fusion
  1.9 0.1 reshape.105
  2.0 0.1 copy.14
  2.0 0.6 pad.4
  2.7 26.6 %swap_requests.1 = s32[16,8,1,128]{3,2,1,0:T(1,128)} custom-call(s32[8,1,128]{2,1,0:T(1,128)} %bitcast.46), custom_call_target="tpu_custom_call" | custom-call | tf_op jit(solution)/shard_map/swap_requests/pallas_call | solution.py:476
  29.3 3.3 dynamic-slice_reduce_fusion
  32.6 0.1 reshape.112
  32.7 1.1 pad_maximum_fusion
  33.8 3.3 gather_fusion
  37.1 0.0 copy-start.2
  37.1 0.0 copy-start
  37.1 0.0 copy-start.1
  37.1 13.7 %all-to-all-start = ((bf16[128,130,128]{2,1,0:T(8,128)(2,1)}), bf16[128,130,128]{2,1,0:T(8,128)(2,1)}, u32[]{:S(2)}, u32[]{:S(2)}) async-start(bf16[128,130,128]{2,1,0:T(8,128)(2,1)} %gather_fusion), calls=%async_computation | async-start | bytes 8912896 | tf_op jit(solution)/shard_map/all_to_all | solution.py:529
  50.8 0.1 div.33
  50.9 0.0 copy-done.2
  50.9 0.6 sub.24.table
  51.6 0.1 and.35
  51.6 0.0 copy-done
  51.7 0.0 copy-done.1
  51.7 0.6 fusion.1
  52.3 10.8 %near_kernel.1 = (bf16[12,13,128,128]{3,2,1,0:T(8,128)(2,1)}, f32[12,1,128]{2,1,0:T(1,128)}, f32[12,1,128]{2,1,0:T(1,128)}) custom-call(s32[192]{0:T(256)} %sub.24.table, s32[12]{0:T(128)} %bitcast.47, bf16[12,128,128]{2,1,0:T(8,128)(2,1)} %bitcast.27, f32[12,1,128]{2,1,0:T(1,128)} %get-tuple-element.33.band), custom_call_target="tpu_custom_call" | custom-call | flops 1022361600 | bytes 10223616 | tf_op jit(solution)/shard_map/near_kernel/pallas_call | solution.py:83
  63.1 183.0 %all-to-all-done = bf16[128,130,128]{2,1,0:T(8,128)(2,1)} async-done(((bf16[128,130,128]{2,1,0:T(8,128)(2,1)}), bf16[128,130,128]{2,1,0:T(8,128)(2,1)}, u32[]{:S(2)}, u32[]{:S(2)}) %all-to-all-start) | async-done | bytes 4259872 | tf_op jit(solution)/shard_map/all_to_all | solution.py:529
  246.1 4.2 gather_fusion.1
  250.3 4.8 %far_kernel.1 = (bf16[12,3,128,128]{3,2,1,0:T(8,128)(2,1)}, f32[12,1,128]{2,1,0:T(1,128)}) custom-call(s32[12]{0:T(128)} %bitcast.48, bf16[12,128,128]{2,1,0:T(8,128)(2,1)} %bitcast.28, f32[12,1,128]{2,1,0:T(1,128)} %get-tuple-element.33.band, bf16[36,130,128]{2,1,0:T(8,128)(2,1)} %gather_fusion.1, f32[12,1,128]{2,1,0:T(1,128)} %get-tuple-element.16.norm_a, ...), custom_call_target="tpu_custom_call" | custom-call | tf_op jit(solution)/shard_map/far_kernel/pallas_call | solution.py:128
  255.1 0.7 convert_element_type.10
  255.8 0.7 gather_fusion.2
  256.5 0.7 copy.15
  257.2 12.6 %all-to-all-start.1 = ((bf16[128,1,128]{2,1,0:T(2,128)(2,1)}), bf16[128,1,128]{2,1,0:T(2,128)(2,1)S(1)}, u32[]{:S(2)}, u32[]{:S(2)}) async-start(bf16[128,1,128]{2,1,0:T(2,128)(2,1)} %copy.15), calls=%async_computation.1 | async-start | bytes 131072 | tf_op jit(solution)/shard_map/all_to_all | solution.py:529
  269.8 8.0 %near_walk.1.partial = f32[12,80,128]{2,1,0:T(8,128)} custom-call(s32[192]{0:T(256)} %sub.24.table, bf16[12,128,128]{2,1,0:T(8,128)(2,1)} %bitcast.29, f32[12,1,128]{2,1,0:T(1,128)} %get-tuple-element.32.prior, f32[12,1,128]{2,1,0:T(1,128)} %get-tuple-element.18.inverse, bf16[64,128]{1,0:T(8,128)(2,1)} %bitcast.37, ...), custom_call_target="tpu_custom_call" | custom-call | flops 408944640 | bytes 10223616 | tf_op jit(solution)/shard_map/near_walk/pallas_call | solution.py:183
  277.8 6.8 %all-to-all-done.1 = bf16[128,1,128]{2,1,0:T(2,128)(2,1)S(1)} async-done(((bf16[128,1,128]{2,1,0:T(2,128)(2,1)}), bf16[128,1,128]{2,1,0:T(2,128)(2,1)S(1)}, u32[]{:S(2)}, u32[]{:S(2)}) %all-to-all-start.1) | async-done | bytes 32800 | tf_op jit(solution)/shard_map/all_to_all | solution.py:529
  284.7 0.6 gather_fusion.3
  285.2 0.6 reshape.162.inverse
  285.9 6.1 %far_walk.1 = (f32[64,1536]{1,0:T(8,128)}, bf16[12,64,128]{2,1,0:T(8,128)(2,1)}, f32[12,1,128]{2,1,0:T(1,128)}, f32[64,64]{1,0:T(8,128)}) custom-call(bf16[36,130,128]{2,1,0:T(8,128)(2,1)} %gather_fusion.1, f32[36,1,128]{2,1,0:T(1,128)} %reshape.162.inverse, bf16[64,128]{1,0:T(8,128)(2,1)} %bitcast.38, ...), custom_call_target="tpu_custom_call" | custom-call | tf_op jit(solution)/shard_map/far_walk/pallas_call | solution.py:237
  292.0 3.1 gather_fusion.4
  295.1 9.3 %all-to-all-start.2 = ((bf16[128,64,128]{2,1,0:T(8,128)(2,1)}), bf16[128,64,128]{2,1,0:T(8,128)(2,1)S(1)}, u32[]{:S(2)}, u32[]{:S(2)}) async-start(bf16[128,64,128]{2,1,0:T(8,128)(2,1)} %gather_fusion.4), calls=%async_computation.2 | async-start | bytes 4194304 | tf_op jit(solution)/shard_map/all_to_all | solution.py:529
  304.4 109.5 %gram_reduce.2 = f32[8,8,64]{2,1,0:T(8,128)} custom-call(f32[8,8,64]{2,1,0:T(8,128)} %bitcast.39), custom_call_target="tpu_custom_call" | custom-call | tf_op jit(solution)/shard_map/gram_reduce/pallas_call | solution.py:502
  413.9 12.4 %near_apply.1 = (f32[64,1536]{1,0:T(8,128)}, f32[12,64,128]{2,1,0:T(8,128)}, f32[64,64]{1,0:T(8,128)}) custom-call(s32[192]{0:T(256)} %sub.24.table, f32[64,64]{1,0:T(8,128)} %bitcast.32, f32[64,1536]{1,0:T(8,128)} %get-tuple-element.22.raw, f32[12,1,128]{2,1,0:T(1,128)} %get-tuple-element.18.inverse, bf16[12,13,128,128]{3,2,1,0:T(8,128)(2,1)} %get-tuple-element.20.kernel_half), custom_call_target="tpu_custom_call" | custom-call | flops 327155712 | bytes 10223616 | tf_op jit(solution)/shard_map/near_apply/pallas_call | solution.py:319
  426.3 0.0 all-to-all-done.2
  426.3 1.5 gather_fusion.5
  427.8 6.0 %far_apply.1 = (f32[64,1536]{1,0:T(8,128)}, f32[64,64]{1,0:T(8,128)}) custom-call(f32[64,64]{1,0:T(8,128)} %get-tuple-element.24.lower_inverse, bf16[36,64,128]{2,1,0:T(8,128)(2,1)} %gather_fusion.5, f32[36,1,128]{2,1,0:T(1,128)} %reshape.162.inverse, f32[12,1,128]{2,1,0:T(1,128)} %get-tuple-element.26.degree, ...), custom_call_target="tpu_custom_call" | custom-call | tf_op jit(solution)/shard_map/far_apply/pallas_call | solution.py:367
  433.8 28.2 %gram_reduce.3 = f32[8,8,64]{2,1,0:T(8,128)} custom-call(f32[8,8,64]{2,1,0:T(8,128)} %bitcast.40), custom_call_target="tpu_custom_call" | custom-call | tf_op jit(solution)/shard_map/gram_reduce/pallas_call | solution.py:502
  462.0 7.6 %finish.1 = f32[64,1536]{1,0:T(8,128)} custom-call(f32[64,64]{1,0:T(8,128)} %bitcast.34, f32[64,1536]{1,0:T(8,128)} %get-tuple-element.29.raw), custom_call_target="tpu_custom_call" | custom-call | tf_op jit(solution)/shard_map/finish/pallas_call | solution.py:277
  (8 shorter events, 0.1 us)
Async XLA Ops:
  37.1 13.8 %copy-start.2 = (s32[1,12,16]{2,0,1:T(1,128)S(1)}, s32[1,12,16]{2,0,1:T(1,128)}, u32[]{:S(2)}) copy-start(s32[1,12,16]{2,0,1:T(1,128)} %param.9) | copy-start | bytes 2308
  37.1 14.5 %copy-start = (bf16[1,1536]{1,0:T(2,128)(2,1)S(1)}, bf16[1,1536]{1,0:T(2,128)(2,1)}, u32[]{:S(2)}) copy-start(bf16[1,1536]{1,0:T(2,128)(2,1)} %param.8) | copy-start | bytes 9220
  37.1 14.5 %copy-start.1 = (bf16[1,1536]{1,0:T(2,128)(2,1)S(1)}, bf16[1,1536]{1,0:T(2,128)(2,1)}, u32[]{:S(2)}) copy-start(bf16[1,1536]{1,0:T(2,128)(2,1)} %param.7) | copy-start | bytes 9220
  37.1 209.0 %all-to-all-start = ((bf16[128,130,128]{2,1,0:T(8,128)(2,1)}), bf16[128,130,128]{2,1,0:T(8,128)(2,1)}, u32[]{:S(2)}, u32[]{:S(2)}) async-start(bf16[128,130,128]{2,1,0:T(8,128)(2,1)} %gather_fusion), calls=%async_computation | async-start | bytes 8912896 | tf_op jit(solution)/shard_map/all_to_all | solution.py:529
  257.2 27.4 %all-to-all-start.1 = ((bf16[128,1,128]{2,1,0:T(2,128)(2,1)}), bf16[128,1,128]{2,1,0:T(2,128)(2,1)S(1)}, u32[]{:S(2)}, u32[]{:S(2)}) async-start(bf16[128,1,128]{2,1,0:T(2,128)(2,1)} %copy.15), calls=%async_computation.1 | async-start | bytes 131072 | tf_op jit(solution)/shard_map/all_to_all | solution.py:529
  295.1 131.2 %all-to-all-start.2 = ((bf16[128,64,128]{2,1,0:T(8,128)(2,1)}), bf16[128,64,128]{2,1,0:T(8,128)(2,1)S(1)}, u32[]{:S(2)}, u32[]{:S(2)}) async-start(bf16[128,64,128]{2,1,0:T(8,128)(2,1)} %gather_fusion.4), calls=%async_computation.2 | async-start | bytes 4194304 | tf_op jit(solution)/shard_map/all_to_all | solution.py:529

commit v7 on v6

--- a/solution.py
+++ b/solution.py
@@ -310,7 +310,7 @@
         partial[tile] = total
         return carry
 
-    lax.fori_loop(0, tiles, one_tile, 0)
+    lax.fori_loop(0, tiles, one_tile, 0, unroll=2)
 
 
 def near_apply(table, gram, raw, inverse, kernel_half, slots, total_rows):

time: 471 us -> 470 us (level)
  no operation moved by 1% of the time
where the time goes in v7:
time: 470 us; the launch traced here: 469 us
  Pallas kernels  219 us (47%)
  waiting for transfers between devices  190 us (40%)
  starting transfers between devices  35.6 us (8%)
  local copies, waits for them, and re-layouts  21.2 us (5%)
    all_to_all x3, waiting for transfers between devices, exchange_tiles(): got = lax.all_to_all(sent, 'rows', split_axis=0, concat_axis=0, tiled=True)  190 us
    pallas_call x2, Pallas kernels, total_gram(): pl.pallas_call(functools.partial(reduce_body, nz, ny), out_shape=jax.Shap...  138 us
    all_to_all x3, starting transfers between devices, exchange_tiles(): got = lax.all_to_all(sent, 'rows', split_axis=0, concat_axis=0, tiled=True)  35.6 us
    pallas_call x1, Pallas kernels, swap_requests(): pl.pallas_call(functools.partial(request_body, nz), out_shape=jax.ShapeDt...  26.6 us
    pallas_call x1, Pallas kernels, near_apply(): pl.pallas_call(functools.partial(near_apply_body, tiles, slots, total_row...  11.4 us
    pallas_call x1, Pallas kernels, near_kernel(): pl.pallas_call(functools.partial(near_kernel_body, tiles, slots), out_sha...  10.8 us
  transfers between devices with their start and end apart: 3, of which 2 were waited for; matrix products, arithmetic and copies ran while one was open for 0% of the time, Pallas kernels for 30%

profile of v7, /device:TPU:1, one launch (start us, length us, event | category | flops | bytes accessed | tf_op | source)
XLA Modules:
  0.0 468.6 jit_solution(8757305060990387728)
XLA Ops:
  0.6 0.7 copy.23
  1.3 0.1 slice_divide_fusion
  1.4 0.1 compare_and_fusion
  1.5 0.1 div.29
  1.6 0.1 ne.64
  1.7 0.1 rem.45
  1.8 0.1 select_reduce_fusion
  1.9 0.1 reshape.105
  2.0 0.1 copy.14
  2.0 0.6 pad.4
  2.7 26.6 %swap_requests.1 = s32[16,8,1,128]{3,2,1,0:T(1,128)} custom-call(s32[8,1,128]{2,1,0:T(1,128)} %bitcast.46), custom_call_target="tpu_custom_call" | custom-call | tf_op jit(solution)/shard_map/swap_requests/pallas_call | solution.py:476
  29.3 3.3 dynamic-slice_reduce_fusion
  32.6 0.1 reshape.112
  32.7 1.1 pad_maximum_fusion
  33.8 3.3 gather_fusion
  37.1 0.0 copy-start.2
  37.1 0.0 copy-start
  37.1 0.0 copy-start.1
  37.1 13.7 %all-to-all-start = ((bf16[128,130,128]{2,1,0:T(8,128)(2,1)}), bf16[128,130,128]{2,1,0:T(8,128)(2,1)}, u32[]{:S(2)}, u32[]{:S(2)}) async-start(bf16[128,130,128]{2,1,0:T(8,128)(2,1)} %gather_fusion), calls=%async_computation | async-start | bytes 8912896 | tf_op jit(solution)/shard_map/all_to_all | solution.py:529
  50.8 0.1 div.33
  50.9 0.0 copy-done.2
  50.9 0.6 sub.24.table
  51.6 0.1 and.35
  51.6 0.0 copy-done
  51.7 0.0 copy-done.1
  51.7 0.6 fusion.1
  52.3 10.8 %near_kernel.1 = (bf16[12,13,128,128]{3,2,1,0:T(8,128)(2,1)}, f32[12,1,128]{2,1,0:T(1,128)}, f32[12,1,128]{2,1,0:T(1,128)}) custom-call(s32[192]{0:T(256)} %sub.24.table, s32[12]{0:T(128)} %bitcast.47, bf16[12,128,128]{2,1,0:T(8,128)(2,1)} %bitcast.27, f32[12,1,128]{2,1,0:T(1,128)} %get-tuple-element.33.band), custom_call_target="tpu_custom_call" | custom-call | flops 1022361600 | bytes 10223616 | tf_op jit(solution)/shard_map/near_kernel/pallas_call | solution.py:83
  63.1 183.0 %all-to-all-done = bf16[128,130,128]{2,1,0:T(8,128)(2,1)} async-done(((bf16[128,130,128]{2,1,0:T(8,128)(2,1)}), bf16[128,130,128]{2,1,0:T(8,128)(2,1)}, u32[]{:S(2)}, u32[]{:S(2)}) %all-to-all-start) | async-done | bytes 4259872 | tf_op jit(solution)/shard_map/all_to_all | solution.py:529
  246.1 4.2 gather_fusion.1
  250.3 4.8 %far_kernel.1 = (bf16[12,3,128,128]{3,2,1,0:T(8,128)(2,1)}, f32[12,1,128]{2,1,0:T(1,128)}) custom-call(s32[12]{0:T(128)} %bitcast.48, bf16[12,128,128]{2,1,0:T(8,128)(2,1)} %bitcast.28, f32[12,1,128]{2,1,0:T(1,128)} %get-tuple-element.33.band, bf16[36,130,128]{2,1,0:T(8,128)(2,1)} %gather_fusion.1, f32[12,1,128]{2,1,0:T(1,128)} %get-tuple-element.16.norm_a, ...), custom_call_target="tpu_custom_call" | custom-call | tf_op jit(solution)/shard_map/far_kernel/pallas_call | solution.py:128
  255.1 0.7 convert_element_type.10
  255.8 0.7 gather_fusion.2
  256.5 0.7 copy.15
  257.2 12.6 %all-to-all-start.1 = ((bf16[128,1,128]{2,1,0:T(2,128)(2,1)}), bf16[128,1,128]{2,1,0:T(2,128)(2,1)S(1)}, u32[]{:S(2)}, u32[]{:S(2)}) async-start(bf16[128,1,128]{2,1,0:T(2,128)(2,1)} %copy.15), calls=%async_computation.1 | async-start | bytes 131072 | tf_op jit(solution)/shard_map/all_to_all | solution.py:529
  269.8 8.0 %near_walk.1.partial = f32[12,80,128]{2,1,0:T(8,128)} custom-call(s32[192]{0:T(256)} %sub.24.table, bf16[12,128,128]{2,1,0:T(8,128)(2,1)} %bitcast.29, f32[12,1,128]{2,1,0:T(1,128)} %get-tuple-element.32.prior, f32[12,1,128]{2,1,0:T(1,128)} %get-tuple-element.18.inverse, bf16[64,128]{1,0:T(8,128)(2,1)} %bitcast.37, ...), custom_call_target="tpu_custom_call" | custom-call | flops 408944640 | bytes 10223616 | tf_op jit(solution)/shard_map/near_walk/pallas_call | solution.py:183
  277.8 6.8 %all-to-all-done.1 = bf16[128,1,128]{2,1,0:T(2,128)(2,1)S(1)} async-done(((bf16[128,1,128]{2,1,0:T(2,128)(2,1)}), bf16[128,1,128]{2,1,0:T(2,128)(2,1)S(1)}, u32[]{:S(2)}, u32[]{:S(2)}) %all-to-all-start.1) | async-done | bytes 32800 | tf_op jit(solution)/shard_map/all_to_all | solution.py:529
  284.6 0.6 gather_fusion.3
  285.2 0.6 reshape.162.inverse
  285.9 6.1 %far_walk.1 = (f32[64,1536]{1,0:T(8,128)}, bf16[12,64,128]{2,1,0:T(8,128)(2,1)}, f32[12,1,128]{2,1,0:T(1,128)}, f32[64,64]{1,0:T(8,128)}) custom-call(bf16[36,130,128]{2,1,0:T(8,128)(2,1)} %gather_fusion.1, f32[36,1,128]{2,1,0:T(1,128)} %reshape.162.inverse, bf16[64,128]{1,0:T(8,128)(2,1)} %bitcast.38, ...), custom_call_target="tpu_custom_call" | custom-call | tf_op jit(solution)/shard_map/far_walk/pallas_call | solution.py:237
  292.0 3.1 gather_fusion.4
  295.1 9.3 %all-to-all-start.2 = ((bf16[128,64,128]{2,1,0:T(8,128)(2,1)}), bf16[128,64,128]{2,1,0:T(8,128)(2,1)S(1)}, u32[]{:S(2)}, u32[]{:S(2)}) async-start(bf16[128,64,128]{2,1,0:T(8,128)(2,1)} %gather_fusion.4), calls=%async_computation.2 | async-start | bytes 4194304 | tf_op jit(solution)/shard_map/all_to_all | solution.py:529
  304.4 109.5 %gram_reduce.2 = f32[8,8,64]{2,1,0:T(8,128)} custom-call(f32[8,8,64]{2,1,0:T(8,128)} %bitcast.39), custom_call_target="tpu_custom_call" | custom-call | tf_op jit(solution)/shard_map/gram_reduce/pallas_call | solution.py:502
  413.9 11.4 %near_apply.1 = (f32[64,1536]{1,0:T(8,128)}, f32[12,64,128]{2,1,0:T(8,128)}, f32[64,64]{1,0:T(8,128)}) custom-call(s32[192]{0:T(256)} %sub.24.table, f32[64,64]{1,0:T(8,128)} %bitcast.32, f32[64,1536]{1,0:T(8,128)} %get-tuple-element.22.raw, f32[12,1,128]{2,1,0:T(1,128)} %get-tuple-element.18.inverse, bf16[12,13,128,128]{3,2,1,0:T(8,128)(2,1)} %get-tuple-element.20.kernel_half), custom_call_target="tpu_custom_call" | custom-call | flops 327155712 | bytes 10223616 | tf_op jit(solution)/shard_map/near_apply/pallas_call | solution.py:319
  425.4 0.0 all-to-all-done.2
  425.4 1.5 gather_fusion.5
  426.9 6.0 %far_apply.1 = (f32[64,1536]{1,0:T(8,128)}, f32[64,64]{1,0:T(8,128)}) custom-call(f32[64,64]{1,0:T(8,128)} %get-tuple-element.24.lower_inverse, bf16[36,64,128]{2,1,0:T(8,128)(2,1)} %gather_fusion.5, f32[36,1,128]{2,1,0:T(1,128)} %reshape.162.inverse, f32[12,1,128]{2,1,0:T(1,128)} %get-tuple-element.26.degree, ...), custom_call_target="tpu_custom_call" | custom-call | tf_op jit(solution)/shard_map/far_apply/pallas_call | solution.py:367
  432.9 28.1 %gram_reduce.3 = f32[8,8,64]{2,1,0:T(8,128)} custom-call(f32[8,8,64]{2,1,0:T(8,128)} %bitcast.40), custom_call_target="tpu_custom_call" | custom-call | tf_op jit(solution)/shard_map/gram_reduce/pallas_call | solution.py:502
  461.0 7.6 %finish.1 = f32[64,1536]{1,0:T(8,128)} custom-call(f32[64,64]{1,0:T(8,128)} %bitcast.34, f32[64,1536]{1,0:T(8,128)} %get-tuple-element.29.raw), custom_call_target="tpu_custom_call" | custom-call | tf_op jit(solution)/shard_map/finish/pallas_call | solution.py:277
  (8 shorter events, 0.1 us)
Async XLA Ops:
  37.1 13.8 %copy-start.2 = (s32[1,12,16]{2,0,1:T(1,128)S(1)}, s32[1,12,16]{2,0,1:T(1,128)}, u32[]{:S(2)}) copy-start(s32[1,12,16]{2,0,1:T(1,128)} %param.9) | copy-start | bytes 2308
  37.1 14.5 %copy-start = (bf16[1,1536]{1,0:T(2,128)(2,1)S(1)}, bf16[1,1536]{1,0:T(2,128)(2,1)}, u32[]{:S(2)}) copy-start(bf16[1,1536]{1,0:T(2,128)(2,1)} %param.8) | copy-start | bytes 9220
  37.1 14.5 %copy-start.1 = (bf16[1,1536]{1,0:T(2,128)(2,1)S(1)}, bf16[1,1536]{1,0:T(2,128)(2,1)}, u32[]{:S(2)}) copy-start(bf16[1,1536]{1,0:T(2,128)(2,1)} %param.7) | copy-start | bytes 9220
  37.1 209.0 %all-to-all-start = ((bf16[128,130,128]{2,1,0:T(8,128)(2,1)}), bf16[128,130,128]{2,1,0:T(8,128)(2,1)}, u32[]{:S(2)}, u32[]{:S(2)}) async-start(bf16[128,130,128]{2,1,0:T(8,128)(2,1)} %gather_fusion), calls=%async_computation | async-start | bytes 8912896 | tf_op jit(solution)/shard_map/all_to_all | solution.py:529
  257.2 27.4 %all-to-all-start.1 = ((bf16[128,1,128]{2,1,0:T(2,128)(2,1)}), bf16[128,1,128]{2,1,0:T(2,128)(2,1)S(1)}, u32[]{:S(2)}, u32[]{:S(2)}) async-start(bf16[128,1,128]{2,1,0:T(2,128)(2,1)} %copy.15), calls=%async_computation.1 | async-start | bytes 131072 | tf_op jit(solution)/shard_map/all_to_all | solution.py:529
  295.1 130.3 %all-to-all-start.2 = ((bf16[128,64,128]{2,1,0:T(8,128)(2,1)}), bf16[128,64,128]{2,1,0:T(8,128)(2,1)S(1)}, u32[]{:S(2)}, u32[]{:S(2)}) async-start(bf16[128,64,128]{2,1,0:T(8,128)(2,1)} %gather_fusion.4), calls=%async_computation.2 | async-start | bytes 4194304 | tf_op jit(solution)/shard_map/all_to_all | solution.py:529
